TPU v7x, 32 devices: a whole 2x2x4 slice. The times are simulated.
32 devices in a mesh: dp: 32 (over z, y, x, core).
Axes of the slice: x: 2, y: 2, z: 4, core: 2. Of those that a mesh axis runs over, the one named last changes fastest.
Arguments:
- layer_input: bfloat16 [4096, 768], P('dp'), may hold values from -6 to 6
- encoder_states: bfloat16 [2048, 768], P('dp'), may hold values from -6 to 6
- output_grad: bfloat16 [4096, 768], P('dp'), may hold values from -6 to 6
- self_query: bfloat16 [768, 768], P('dp'), may hold values from -0.078125 to 0.078125
- self_key: bfloat16 [768, 768], P('dp'), may hold values from -0.21875 to 0.21875
- self_value: bfloat16 [768, 768], P('dp'), may hold values from -0.21875 to 0.21875
- self_output: bfloat16 [768, 768], P('dp'), may hold values from -0.625 to 0.625
- cross_query: bfloat16 [768, 768], P('dp'), may hold values from -0.078125 to 0.078125
- cross_key: bfloat16 [768, 768], P('dp'), may hold values from -0.21875 to 0.21875
- cross_value: bfloat16 [768, 768], P('dp'), may hold values from -0.21875 to 0.21875
- cross_output: bfloat16 [768, 768], P('dp'), may hold values from -0.625 to 0.625
- feed_gate: bfloat16 [768, 2048], P('dp'), may hold values from -0.21875 to 0.21875
- feed_up: bfloat16 [768, 2048], P('dp'), may hold values from -0.21875 to 0.21875
- feed_down: bfloat16 [2048, 768], P('dp'), may hold values from -0.125 to 0.125
- gain_self: bfloat16 [768], P('dp'), may hold values from 0.5 to 1.5
- gain_cross: bfloat16 [768], P('dp'), may hold values from 0.5 to 1.5
- gain_feed: bfloat16 [768], P('dp'), may hold values from 0.5 to 1.5
- bias_table: float32 [32, 12], replicated, may hold values from -4 to 4
- target_lengths: int32 [32, 4], P('dp'), may hold values from 1 to 80, 128 in all within a row
- source_lengths: int32 [32, 4], P('dp'), may hold values from 1 to 32, 64 in all within a row
- distance_bucket: int32 [80], replicated, may hold values from 0 to 31
Outputs:
- layer_output: bfloat16 [4096, 768], P('dp')
- input_grad: float32 [4096, 768], P('dp')
- encoder_grad: float32 [2048, 768], P('dp')
- grad_self_query: float32 [768, 768], P('dp')
- grad_self_key: float32 [768, 768], P('dp')
- grad_self_value: float32 [768, 768], P('dp')
- grad_self_output: float32 [768, 768], P('dp')
- grad_cross_query: float32 [768, 768], P('dp')
- grad_cross_key: float32 [768, 768], P('dp')
- grad_cross_value: float32 [768, 768], P('dp')
- grad_cross_output: float32 [768, 768], P('dp')
- grad_feed_gate: float32 [768, 2048], P('dp')
- grad_feed_up: float32 [768, 2048], P('dp')
- grad_feed_down: float32 [2048, 768], P('dp')
- grad_gain_self: float32 [768], P('dp')
- grad_gain_cross: float32 [768], P('dp')
- grad_gain_feed: float32 [768], P('dp')
- grad_bias_table: float32 [32, 12], replicated
Inputs may be any that keep to these rules, and one draw needn't show every extreme that they name: `target_lengths`: each row lists the lengths of the 4 decoder sequences of one device in the order of its rows and sums to 128. `source_lengths`: each row lists the lengths of the encoder sequences of the same 4 sequences and sums to 64.
All inputs are finite; a program needn't handle non-finite values.
Results may differ from a plain program's by a relative error of at most 0.03.
The roundings to bfloat16 on the way count: a program that leaves them out, or rounds other values in their place, can miss the bound.
Values may be sent and summed in bfloat16 or wider, within the bound.
No kernel may reach another device: no remote copies, remote signals or barrier semaphores. Data moves between devices by JAX's collectives and lax.ppermute only.
A program may use at most 192 MiB of HBM per device.

v0:
```python
import jax
import jax.numpy as jnp
from jax import lax
from jax.sharding import PartitionSpec as P

H = 12


EPSILON = 1e-06
MASKED = -1e30


def matmul(left, right):
    return jnp.dot(left, right, preferred_element_type=jnp.float32)


def rms_norm(hidden, gain_row):
    norm_scale = lax.rsqrt(jnp.mean(hidden * hidden, axis=-1, keepdims=True) + EPSILON)
    return hidden * norm_scale * gain_row


def gated_gelu(gate_part, linear_part):
    return jax.nn.gelu(gate_part, approximate=True) * linear_part


def toeplitz(vector):
    length = vector.shape[0]
    padded = jnp.concatenate([vector[::-1], jnp.zeros((length,), vector.dtype)])
    flattened = jnp.tile(padded, length + 1)[length - 1 : length - 1 + length * (2 * length - 1)]
    return flattened.reshape(length, 2 * length - 1)[:, :length]


def segment_ids(lengths, row_total):
    boundary = jnp.cumsum(lengths)
    row_index = jnp.arange(row_total, dtype=jnp.int32)
    return jnp.sum((row_index[:, None] >= boundary[None, :]).astype(jnp.int32), axis=1)


def heads_first(matrix):
    return matrix.reshape(matrix.shape[0], H, -1).transpose(1, 0, 2)


def heads_last(tensor):
    return tensor.transpose(1, 0, 2).reshape(tensor.shape[1], -1)


def head_scores(query_head, key_head, bias_block, allowed):
    scores = matmul(query_head, key_head.T)
    if bias_block is not None:
        scores = scores + bias_block
    return jnp.where(allowed, scores, MASKED)


def head_forward(query_head, key_head, value_head, bias_block, allowed):
    scores = head_scores(query_head, key_head, bias_block, allowed)
    highest = jnp.max(scores, axis=1, keepdims=True)
    exp_total = jnp.sum(jnp.exp(scores - highest), axis=1, keepdims=True)
    log_total = highest + jnp.log(exp_total)
    weights = jnp.exp(scores - log_total).astype(jnp.bfloat16)
    mixed_rows = matmul(weights, value_head).astype(jnp.bfloat16)
    return (mixed_rows, log_total[:, 0])


def head_backward(
    query_head, key_head, value_head, mixed_head, grad_head, log_total, bias_block, allowed
):
    scores = head_scores(query_head, key_head, bias_block, allowed)
    weights = jnp.where(allowed, jnp.exp(scores - log_total[:, None]), 0.0)
    low_weights = weights.astype(jnp.bfloat16)
    grad_weights = matmul(grad_head, value_head.T)
    row_dot = jnp.sum(
        grad_head.astype(jnp.float32) * mixed_head.astype(jnp.float32), axis=1, keepdims=True
    )
    grad_scores = weights * (grad_weights - row_dot)
    low_scores = grad_scores.astype(jnp.bfloat16)
    grad_query = matmul(low_scores, key_head).astype(jnp.bfloat16)
    grad_key = matmul(low_scores.T, query_head).astype(jnp.bfloat16)
    grad_value = matmul(low_weights.T, grad_head).astype(jnp.bfloat16)
    return (grad_query, grad_key, grad_value, grad_scores)


def self_attention(query_rows, key_rows, value_rows, bias_rows, allowed):

    def one_head(packed):
        query_head, key_head, value_head, bias_head = packed
        return head_forward(query_head, key_head, value_head, toeplitz(bias_head), allowed)

    mixed_heads, log_total = lax.map(
        one_head,
        (heads_first(query_rows), heads_first(key_rows), heads_first(value_rows), bias_rows),
    )
    return (heads_last(mixed_heads), log_total)


def cross_attention(query_rows, key_rows, value_rows, allowed):

    def one_head(packed):
        query_head, key_head, value_head = packed
        return head_forward(query_head, key_head, value_head, None, allowed)

    mixed_heads, log_total = lax.map(
        one_head, (heads_first(query_rows), heads_first(key_rows), heads_first(value_rows))
    )
    return (heads_last(mixed_heads), log_total)


def self_attention_grad(
    query_rows, key_rows, value_rows, mixed_rows, grad_rows, log_total, bias_rows, allowed
):

    def one_head(packed):
        query_head, key_head, value_head, mixed_head, grad_head, log_head, bias_head = packed
        bias_block, pullback = jax.vjp(toeplitz, bias_head)
        grad_query, grad_key, grad_value, grad_scores = head_backward(
            query_head, key_head, value_head, mixed_head, grad_head, log_head, bias_block, allowed
        )
        return (grad_query, grad_key, grad_value, pullback(grad_scores)[0])

    grad_query, grad_key, grad_value, grad_bias = lax.map(
        one_head,
        (
            heads_first(query_rows),
            heads_first(key_rows),
            heads_first(value_rows),
            heads_first(mixed_rows),
            heads_first(grad_rows),
            log_total,
            bias_rows,
        ),
    )
    return (heads_last(grad_query), heads_last(grad_key), heads_last(grad_value), grad_bias)


def cross_attention_grad(
    query_rows, key_rows, value_rows, mixed_rows, grad_rows, log_total, allowed
):

    def one_head(packed):
        query_head, key_head, value_head, mixed_head, grad_head, log_head = packed
        grad_query, grad_key, grad_value, grad_scores = head_backward(
            query_head, key_head, value_head, mixed_head, grad_head, log_head, None, allowed
        )
        return (grad_query, grad_key, grad_value)

    grad_query, grad_key, grad_value = lax.map(
        one_head,
        (
            heads_first(query_rows),
            heads_first(key_rows),
            heads_first(value_rows),
            heads_first(mixed_rows),
            heads_first(grad_rows),
            log_total,
        ),
    )
    return (heads_last(grad_query), heads_last(grad_key), heads_last(grad_value))


def bucket_onehot(distance_bucket, buckets):
    return (distance_bucket[:, None] == jnp.arange(buckets, dtype=jnp.int32)[None, :]).astype(
        jnp.float32
    )


def distance_bias(onehot, bias_table, row_count):
    per_distance = jnp.dot(onehot, bias_table, precision=lax.Precision.HIGHEST)
    return jnp.pad(per_distance.T, ((0, 0), (0, row_count - per_distance.shape[0])))


def table_grad(onehot, grad_bias_rows):
    return jnp.dot(
        onehot.T, grad_bias_rows[:, : onehot.shape[0]].T, precision=lax.Precision.HIGHEST
    )


def layer_forward(
    layer_input,
    encoder_states,
    target_lengths,
    source_lengths,
    bias_rows,
    attention_full,
    feed_full,
):
    (
        self_query,
        self_key,
        self_value,
        self_output,
        cross_query,
        cross_key,
        cross_value,
        cross_output,
        gain_self,
        gain_cross,
        gain_feed,
    ) = attention_full
    feed_gate, feed_up, feed_down = feed_full
    row_count = layer_input.shape[0]
    target_segment = segment_ids(target_lengths, row_count)
    source_segment = segment_ids(source_lengths, encoder_states.shape[0])
    position = jnp.arange(row_count, dtype=jnp.int32)
    causal = (target_segment[:, None] == target_segment[None, :]) & (
        position[None, :] <= position[:, None]
    )
    aligned = target_segment[:, None] == source_segment[None, :]
    resid_zero = layer_input.astype(jnp.float32)
    normed_one = rms_norm(resid_zero, gain_self.astype(jnp.float32)).astype(jnp.bfloat16)
    query_rows = matmul(normed_one, self_query).astype(jnp.bfloat16)
    key_rows = matmul(normed_one, self_key).astype(jnp.bfloat16)
    value_rows = matmul(normed_one, self_value).astype(jnp.bfloat16)
    mixed_one, log_one = self_attention(query_rows, key_rows, value_rows, bias_rows, causal)
    resid_one = resid_zero + matmul(mixed_one, self_output)
    normed_two = rms_norm(resid_one, gain_cross.astype(jnp.float32)).astype(jnp.bfloat16)
    cross_rows = matmul(normed_two, cross_query).astype(jnp.bfloat16)
    cross_keys = matmul(encoder_states, cross_key).astype(jnp.bfloat16)
    cross_values = matmul(encoder_states, cross_value).astype(jnp.bfloat16)
    mixed_two, log_two = cross_attention(cross_rows, cross_keys, cross_values, aligned)
    resid_two = resid_one + matmul(mixed_two, cross_output)
    normed_three = rms_norm(resid_two, gain_feed.astype(jnp.float32)).astype(jnp.bfloat16)
    gate_part = matmul(normed_three, feed_gate)
    linear_part = matmul(normed_three, feed_up)
    hidden = gated_gelu(gate_part, linear_part).astype(jnp.bfloat16)
    layer_output = (resid_two + matmul(hidden, feed_down)).astype(jnp.bfloat16)
    saved_state = (
        causal,
        aligned,
        resid_zero,
        normed_one,
        query_rows,
        key_rows,
        value_rows,
        mixed_one,
        log_one,
        resid_one,
        normed_two,
        cross_rows,
        cross_keys,
        cross_values,
        mixed_two,
        log_two,
        resid_two,
        normed_three,
        gate_part,
        linear_part,
        hidden,
    )
    return (layer_output, saved_state)


def feed_backward(saved_state, output_grad, feed_full, gain_feed):
    feed_gate, feed_up, feed_down = feed_full
    resid_two, normed_three, gate_part, linear_part, hidden = saved_state[16:]
    grad_feed_down = matmul(hidden.T, output_grad)
    grad_hidden = matmul(output_grad, feed_down.T)
    unused_value, pullback = jax.vjp(gated_gelu, gate_part, linear_part)
    grad_gate, grad_linear = pullback(grad_hidden)
    grad_gate = grad_gate.astype(jnp.bfloat16)
    grad_linear = grad_linear.astype(jnp.bfloat16)
    grad_feed_gate = matmul(normed_three.T, grad_gate)
    grad_feed_up = matmul(normed_three.T, grad_linear)
    grad_normed = matmul(grad_gate, feed_gate.T) + matmul(grad_linear, feed_up.T)
    unused_norm, norm_pull = jax.vjp(rms_norm, resid_two, gain_feed.astype(jnp.float32))
    grad_resid_part, grad_gain_feed = norm_pull(grad_normed)
    grad_resid_two = output_grad.astype(jnp.float32) + grad_resid_part
    return ((grad_feed_gate, grad_feed_up, grad_feed_down), grad_gain_feed, grad_resid_two)


def attention_backward(saved_state, grad_resid_two, attention_full, encoder_states, bias_rows):
    (
        causal,
        aligned,
        resid_zero,
        normed_one,
        query_rows,
        key_rows,
        value_rows,
        mixed_one,
        log_one,
        resid_one,
        normed_two,
        cross_rows,
        cross_keys,
        cross_values,
        mixed_two,
        log_two,
    ) = saved_state[:16]
    (
        self_query,
        self_key,
        self_value,
        self_output,
        cross_query,
        cross_key,
        cross_value,
        cross_output,
        gain_self,
        gain_cross,
        gain_feed,
    ) = attention_full
    low_two = grad_resid_two.astype(jnp.bfloat16)
    grad_cross_output = matmul(mixed_two.T, low_two)
    grad_mixed_two = matmul(low_two, cross_output.T).astype(jnp.bfloat16)
    grad_cross_rows, grad_cross_keys, grad_cross_values = cross_attention_grad(
        cross_rows, cross_keys, cross_values, mixed_two, grad_mixed_two, log_two, aligned
    )
    grad_cross_query = matmul(normed_two.T, grad_cross_rows)
    grad_cross_key = matmul(encoder_states.T, grad_cross_keys)
    grad_cross_value = matmul(encoder_states.T, grad_cross_values)
    encoder_grad = matmul(grad_cross_keys, cross_key.T) + matmul(grad_cross_values, cross_value.T)
    grad_normed_two = matmul(grad_cross_rows, cross_query.T)
    unused_two, pull_two = jax.vjp(rms_norm, resid_one, gain_cross.astype(jnp.float32))
    grad_part_two, grad_gain_cross = pull_two(grad_normed_two)
    grad_resid_one = grad_resid_two + grad_part_two
    low_one = grad_resid_one.astype(jnp.bfloat16)
    grad_self_output = matmul(mixed_one.T, low_one)
    grad_mixed_one = matmul(low_one, self_output.T).astype(jnp.bfloat16)
    grad_query_rows, grad_key_rows, grad_value_rows, grad_bias_rows = self_attention_grad(
        query_rows, key_rows, value_rows, mixed_one, grad_mixed_one, log_one, bias_rows, causal
    )
    grad_self_query = matmul(normed_one.T, grad_query_rows)
    grad_self_key = matmul(normed_one.T, grad_key_rows)
    grad_self_value = matmul(normed_one.T, grad_value_rows)
    grad_normed_one = (
        matmul(grad_query_rows, self_query.T)
        + matmul(grad_key_rows, self_key.T)
        + matmul(grad_value_rows, self_value.T)
    )
    unused_one, pull_one = jax.vjp(rms_norm, resid_zero, gain_self.astype(jnp.float32))
    grad_part_one, grad_gain_self = pull_one(grad_normed_one)
    input_grad = grad_resid_one + grad_part_one
    matrices = (
        grad_self_query,
        grad_self_key,
        grad_self_value,
        grad_self_output,
        grad_cross_query,
        grad_cross_key,
        grad_cross_value,
        grad_cross_output,
    )
    return (matrices, grad_gain_self, grad_gain_cross, grad_bias_rows, input_grad, encoder_grad)


def body(
    layer_input,
    encoder_states,
    output_grad,
    self_query,
    self_key,
    self_value,
    self_output,
    cross_query,
    cross_key,
    cross_value,
    cross_output,
    feed_gate,
    feed_up,
    feed_down,
    gain_self,
    gain_cross,
    gain_feed,
    bias_table,
    target_lengths,
    source_lengths,
    distance_bucket,
):
    attention_full = (
        lax.all_gather(self_query, "dp", axis=0, tiled=True),
        lax.all_gather(self_key, "dp", axis=0, tiled=True),
        lax.all_gather(self_value, "dp", axis=0, tiled=True),
        lax.all_gather(self_output, "dp", axis=0, tiled=True),
        lax.all_gather(cross_query, "dp", axis=0, tiled=True),
        lax.all_gather(cross_key, "dp", axis=0, tiled=True),
        lax.all_gather(cross_value, "dp", axis=0, tiled=True),
        lax.all_gather(cross_output, "dp", axis=0, tiled=True),
        lax.all_gather(gain_self, "dp", axis=0, tiled=True),
        lax.all_gather(gain_cross, "dp", axis=0, tiled=True),
        lax.all_gather(gain_feed, "dp", axis=0, tiled=True),
    )
    feed_full = (
        lax.all_gather(feed_gate, "dp", axis=0, tiled=True),
        lax.all_gather(feed_up, "dp", axis=0, tiled=True),
        lax.all_gather(feed_down, "dp", axis=0, tiled=True),
    )
    onehot = bucket_onehot(distance_bucket, bias_table.shape[0])
    bias_rows = distance_bias(onehot, bias_table, layer_input.shape[0])
    layer_output, saved_state = layer_forward(
        layer_input,
        encoder_states,
        target_lengths[0],
        source_lengths[0],
        bias_rows,
        attention_full,
        feed_full,
    )
    feed_grads, grad_gain_feed, grad_resid_two = feed_backward(
        saved_state, output_grad, feed_full, attention_full[10]
    )
    feed_shares = (
        lax.psum_scatter(feed_grads[0], "dp", scatter_dimension=0, tiled=True),
        lax.psum_scatter(feed_grads[1], "dp", scatter_dimension=0, tiled=True),
        lax.psum_scatter(feed_grads[2], "dp", scatter_dimension=0, tiled=True),
    )
    matrices, grad_gain_self, grad_gain_cross, grad_bias_rows, input_grad, encoder_grad = (
        attention_backward(saved_state, grad_resid_two, attention_full, encoder_states, bias_rows)
    )
    attention_shares = (
        lax.psum_scatter(matrices[0], "dp", scatter_dimension=0, tiled=True),
        lax.psum_scatter(matrices[1], "dp", scatter_dimension=0, tiled=True),
        lax.psum_scatter(matrices[2], "dp", scatter_dimension=0, tiled=True),
        lax.psum_scatter(matrices[3], "dp", scatter_dimension=0, tiled=True),
        lax.psum_scatter(matrices[4], "dp", scatter_dimension=0, tiled=True),
        lax.psum_scatter(matrices[5], "dp", scatter_dimension=0, tiled=True),
        lax.psum_scatter(matrices[6], "dp", scatter_dimension=0, tiled=True),
        lax.psum_scatter(matrices[7], "dp", scatter_dimension=0, tiled=True),
    )
    shares = tuple(attention_shares) + tuple(feed_shares)
    grad_table, total_self, total_cross, total_feed = lax.psum(
        (table_grad(onehot, grad_bias_rows), grad_gain_self, grad_gain_cross, grad_gain_feed), "dp"
    )
    share_length = gain_self.shape[0]
    share_start = lax.axis_index("dp") * share_length
    own_self = lax.dynamic_slice_in_dim(total_self, share_start, share_length)
    own_cross = lax.dynamic_slice_in_dim(total_cross, share_start, share_length)
    own_feed = lax.dynamic_slice_in_dim(total_feed, share_start, share_length)
    return (
        layer_output,
        input_grad,
        encoder_grad,
        shares[0],
        shares[1],
        shares[2],
        shares[3],
        shares[4],
        shares[5],
        shares[6],
        shares[7],
        shares[8],
        shares[9],
        shares[10],
        own_self,
        own_cross,
        own_feed,
        grad_table,
    )


def solution(mesh):
    return jax.shard_map(
        body,
        mesh=mesh,
        in_specs=(
            P("dp", None),
            P("dp", None),
            P("dp", None),
            P("dp", None),
            P("dp", None),
            P("dp", None),
            P("dp", None),
            P("dp", None),
            P("dp", None),
            P("dp", None),
            P("dp", None),
            P("dp", None),
            P("dp", None),
            P("dp", None),
            P("dp"),
            P("dp"),
            P("dp"),
            P(),
            P("dp", None),
            P("dp", None),
            P(),
        ),
        out_specs=(
            P("dp", None),
            P("dp", None),
            P("dp", None),
            P("dp", None),
            P("dp", None),
            P("dp", None),
            P("dp", None),
            P("dp", None),
            P("dp", None),
            P("dp", None),
            P("dp", None),
            P("dp", None),
            P("dp", None),
            P("dp", None),
            P("dp"),
            P("dp"),
            P("dp"),
            P(),
        ),
        check_vma=False,
    )
```

profile of v0, /device:TPU:0, one launch (start us, length us, event | category | flops | bytes accessed | tf_op | source)
XLA Modules:
  0.0 1905.3 jit_solution(1568029277821795618)
XLA Ops:
  17.3 42.2 %all-reduce.9 = (bf16[768]{0:T(1024)(128)(2,1)S(1)}, bf16[768]{0:T(1024)(128)(2,1)S(1)}, bf16[768]{0:T(1024)(128)(2,1)S(1)}) all-reduce(bf16[768]{0:T(1024)(128)(2,1)S(1)} %dynamic-update-slice, bf16[768]{0:T(1024)(128)(2,1)S(1)} %dynamic-update-slice.1, bf16[768]{0:T(1024)(128)(2,1)S(1)} %dynamic-update-slice.2), channel_id=1, replica_groups=mesh['dp'=32] {'dp'}, use_global_device_ids=true, to_apply=%add.5 | all-reduce | flops 2304 | bytes 9216
  63.4 4.4 all-gather.12.cloned.1.call-done
  67.9 1.7 convolution_convert_fusion.13
  70.0 53.5 %all-gather.14.cloned.1.call-done = bf16[768,768]{1,0:T(8,128)(2,1)} async-done(((bf16[24,768]{1,0:T(8,128)(2,1)}), bf16[768,768]{1,0:T(8,128)(2,1)}) %all-gather.14.cloned.1.call-update) | async-done | bytes 1179664 | tf_op jit(solution)/shard_map/all_gather | solution.py:370
  123.5 1.6 convolution_convert_fusion.12
  125.6 53.7 %all-gather.16.cloned.1.call-done = bf16[768,768]{1,0:T(8,128)(2,1)} async-done(((bf16[24,768]{1,0:T(8,128)(2,1)}), bf16[768,768]{1,0:T(8,128)(2,1)}) %all-gather.16.cloned.1.call-update) | async-done | bytes 1179664 | tf_op jit(solution)/shard_map/all_gather | solution.py:371
  179.3 1.6 convolution_convert_fusion.11
  181.4 14.7 while.58
  196.1 38.9 %all-gather.18.cloned.1.call-done = bf16[768,768]{1,0:T(8,128)(2,1)} async-done(((bf16[24,768]{1,0:T(8,128)(2,1)}), bf16[768,768]{1,0:T(8,128)(2,1)}) %all-gather.18.cloned.1.call-update) | async-done | bytes 1179664 | tf_op jit(solution)/shard_map/all_gather | solution.py:372
  235.0 1.7 multiply_reduce_fusion.5
  236.8 53.9 %all-gather.20.cloned.1.call-done = bf16[768,768]{1,0:T(8,128)(2,1)} async-done(((bf16[24,768]{1,0:T(8,128)(2,1)}), bf16[768,768]{1,0:T(8,128)(2,1)}) %all-gather.20.cloned.1.call-update) | async-done | bytes 1179664 | tf_op jit(solution)/shard_map/all_gather | solution.py:373
  290.6 1.6 convolution_convert_fusion.10
  292.7 53.5 %all-gather.22.cloned.1.call-done = bf16[768,768]{1,0:T(8,128)(2,1)} async-done(((bf16[24,768]{1,0:T(8,128)(2,1)}), bf16[768,768]{1,0:T(8,128)(2,1)}) %all-gather.22.cloned.1.call-update) | async-done | bytes 1179664 | tf_op jit(solution)/shard_map/all_gather | solution.py:374
  346.2 1.6 convolution_convert_fusion.15
  348.1 53.9 %all-gather.24.cloned.1.call-done = bf16[768,768]{1,0:T(8,128)(2,1)} async-done(((bf16[24,768]{1,0:T(8,128)(2,1)}), bf16[768,768]{1,0:T(8,128)(2,1)}) %all-gather.24.cloned.1.call-update) | async-done | bytes 1179664 | tf_op jit(solution)/shard_map/all_gather | solution.py:375
  402.0 1.6 convolution_convert_fusion.14
  403.9 5.9 while.59
  409.8 47.9 %all-gather.26.cloned.1.call-done = bf16[768,768]{1,0:T(8,128)(2,1)} async-done(((bf16[24,768]{1,0:T(8,128)(2,1)}), bf16[768,768]{1,0:T(8,128)(2,1)}) %all-gather.26.cloned.1.call-update) | async-done | bytes 1179664 | tf_op jit(solution)/shard_map/all_gather | solution.py:376
  457.7 1.7 multiply_reduce_fusion.4
  459.6 59.0 %all-gather.28.cloned.1.call-done = bf16[768,2048]{1,0:T(8,128)(2,1)} async-done(((bf16[24,2048]{1,0:T(8,128)(2,1)}), bf16[768,2048]{1,0:T(8,128)(2,1)}) %all-gather.28.cloned.1.call-update) | async-done | bytes 3145744 | tf_op jit(solution)/shard_map/all_gather | solution.py:382
  518.6 3.5 fusion.139
  522.1 57.0 %all-gather.30.cloned.1.call-done = bf16[768,2048]{1,0:T(8,128)(2,1)} async-done(((bf16[24,2048]{1,0:T(8,128)(2,1)}), bf16[768,2048]{1,0:T(8,128)(2,1)}) %all-gather.30.cloned.1.call-update) | async-done | bytes 3145744 | tf_op jit(solution)/shard_map/all_gather | solution.py:383
  579.2 3.4 fusion.140
  582.6 57.3 %all-gather.32.cloned.1.call-done = bf16[2048,768]{1,0:T(8,128)(2,1)} async-done(((bf16[64,768]{1,0:T(8,128)(2,1)}), bf16[2048,768]{1,0:T(8,128)(2,1)}) %all-gather.32.cloned.1.call-update) | async-done | bytes 3145744 | tf_op jit(solution)/shard_map/all_gather | solution.py:384
  639.9 5.0 multiply_convert_fusion
  644.9 1.2 fusion.141
  647.1 1.8 multiply_reduce_fusion
  651.0 55.5 %while.60 = (s32[]{:T(128)}, bf16[12,128,64]{1,2,0:T(8,128)(2,1)S(1)}, bf16[12,64,64]{2,1,0:T(8,128)(2,1)}, bf16[12,64,64]{2,1,0:T(8,128)(2,1)}, bf16[12,128,64]...) while((s32[]{:T(128)}, ...), condition=%wide.region_18.19_spmd.clone, body=%wide.region_16.18_spmd.clone.sunk | while | flops 5357442 | bytes 516485 | solution.py:145
  652.4 1.5 fusion.267
  657.1 1.5 fusion.267
  661.7 1.5 fusion.267
  666.3 1.5 fusion.267
  670.9 1.5 fusion.267
  675.5 1.5 fusion.267
  680.2 1.5 fusion.267
  684.8 1.5 fusion.267
  689.4 1.5 fusion.267
  694.0 1.5 fusion.267
  698.6 1.5 fusion.267
  703.3 1.5 fusion.267
  706.4 2.0 fusion.127
  708.5 1.9 fusion.117
  713.2 1.9 fusion.114
  716.8 2.0 copy.132
  722.5 2.0 copy.134
  724.7 93.5 %while.61 = (s32[]{:T(128)}, bf16[12,128,64]{1,2,0:T(8,128)(2,1)S(1)}, bf16[12,128,64]{1,2,0:T(8,128)(2,1)S(1)}, bf16[12,128,64]{1,2,0:T(8,128)(2,1)S(1)}, f32[1...) while((s32[]{:T(128)}, ...), condition=%wide.region_23.24_spmd.clone, body=%wide.region_20.23_spmd.clone.sunk | while | flops 10772354 | bytes 2920625 | solution.py:119
  818.2 2.0 fusion.132
  820.2 2.0 fusion.130
  822.3 2.0 fusion.128
  825.4 3.6 fusion.144
  830.1 3.6 fusion.145
  834.8 3.6 fusion.146
  842.3 38.5 %all-reduce.8 = (f32[768]{0:T(1024)S(1)}, f32[768]{0:T(1024)S(1)}, f32[768]{0:T(1024)S(1)}, f32[32,12]{0,1:T(8,128)}) all-reduce(f32[768]{0:T(1024)S(1)} %get-tuple-element.559, f32[768]{0:T(1024)S(1)} %get-tuple-element.557, f32[768]{0:T(1024)S(1)} %copy-done.39, f32[32,12]{0,1:T(8,128)S(1)} %fusion.120), channel_id=1, replica_groups=mesh['dp'=32] {'dp'}, use_global_device_ids=true, to_apply=%region_37.38 | all-reduce | flops 2688 | bytes 21504 | tf_op jit(solution)/shard_map/psum | solution.py:419
  885.3 3.2 fusion.97
  888.4 23.4 %reduce-scatter.26.cloned.1.call-done = f32[24,768]{1,0:T(8,128)} async-done(((f32[768,768]{1,0:T(8,128)}), f32[24,768]{1,0:T(8,128)}) %reduce-scatter.26.cloned.1.call-update) | async-done | bytes 73744 | tf_op jit(solution)/shard_map/reduce_scatter | solution.py:416
  911.9 104.3 %reduce-scatter.22.cloned.1.call-done = f32[24,768]{1,0:T(8,128)} async-done(((f32[768,768]{1,0:T(8,128)}), f32[24,768]{1,0:T(8,128)}) %reduce-scatter.22.cloned.1.call-update) | async-done | bytes 73744 | tf_op jit(solution)/shard_map/reduce_scatter | solution.py:412
  1016.1 104.4 %reduce-scatter.34.cloned.1.call-done = f32[24,768]{1,0:T(8,128)} async-done(((f32[768,768]{1,0:T(8,128)}), f32[24,768]{1,0:T(8,128)}) %reduce-scatter.34.cloned.1.call-update) | async-done | bytes 73744
  1120.5 104.2 %reduce-scatter.36.cloned.1.call-done = f32[24,768]{1,0:T(8,128)} async-done(((f32[768,768]{1,0:T(8,128)}), f32[24,768]{1,0:T(8,128)}) %reduce-scatter.36.cloned.1.call-update) | async-done | bytes 73744
  1224.7 104.4 %reduce-scatter.16.cloned.1.call-done = f32[24,768]{1,0:T(8,128)} async-done(((f32[768,768]{1,0:T(8,128)}), f32[24,768]{1,0:T(8,128)}) %reduce-scatter.16.cloned.1.call-update) | async-done | bytes 73744 | tf_op jit(solution)/shard_map/reduce_scatter | solution.py:409
  1329.2 104.4 %reduce-scatter.18.cloned.1.call-done = f32[24,768]{1,0:T(8,128)} async-done(((f32[768,768]{1,0:T(8,128)}), f32[24,768]{1,0:T(8,128)}) %reduce-scatter.18.cloned.1.call-update) | async-done | bytes 73744 | tf_op jit(solution)/shard_map/reduce_scatter | solution.py:410
  1433.5 104.5 %reduce-scatter.20.cloned.1.call-done = f32[24,768]{1,0:T(8,128)} async-done(((f32[768,768]{1,0:T(8,128)}), f32[24,768]{1,0:T(8,128)}) %reduce-scatter.20.cloned.1.call-update) | async-done | bytes 73744 | tf_op jit(solution)/shard_map/reduce_scatter | solution.py:411
  1538.1 120.1 %reduce-scatter.28.cloned.1.call-done = f32[24,2048]{1,0:T(8,128)} async-done(((f32[768,2048]{1,0:T(8,128)}), f32[24,2048]{1,0:T(8,128)}) %reduce-scatter.28.cloned.1.call-update) | async-done | bytes 196624 | tf_op jit(solution)/shard_map/reduce_scatter | solution.py:401
  1658.2 120.1 %reduce-scatter.30.cloned.1.call-done = f32[24,2048]{1,0:T(8,128)} async-done(((f32[768,2048]{1,0:T(8,128)}), f32[24,2048]{1,0:T(8,128)}) %reduce-scatter.30.cloned.1.call-update) | async-done | bytes 196624 | tf_op jit(solution)/shard_map/reduce_scatter | solution.py:402
  1778.4 120.1 %reduce-scatter.32.cloned.1.call-done = f32[64,768]{1,0:T(8,128)} async-done(((f32[2048,768]{1,0:T(8,128)}), f32[64,768]{1,0:T(8,128)}) %reduce-scatter.32.cloned.1.call-update) | async-done | bytes 196624 | tf_op jit(solution)/shard_map/reduce_scatter | solution.py:403
  (832 shorter events, 187.8 us)
Async XLA Ops:
  7.2 339.1 %copy-start = (bf16[64,768]{1,0:T(8,128)(2,1)S(1)}, bf16[64,768]{1,0:T(8,128)(2,1)}, u32[]{:S(2)}) copy-start(bf16[64,768]{1,0:T(8,128)(2,1)} %param.30) | copy-start | bytes 294916
  7.2 60.7 %all-gather.12.cloned.1.call-start = ((), (), s32[]{:S(2)}) async-start(), calls=%async_computation.11 | async-start | bytes 1216512 | tf_op jit(solution)/shard_map/all_gather | solution.py:369
  7.9 115.6 %all-gather.14.cloned.1.call-start = ((), (), s32[]{:S(2)}) async-start(), calls=%async_computation.12 | async-start | bytes 1216512 | tf_op jit(solution)/shard_map/all_gather | solution.py:370
  8.7 170.6 %all-gather.16.cloned.1.call-start = ((), (), s32[]{:S(2)}) async-start(), calls=%async_computation.13 | async-start | bytes 1216512 | tf_op jit(solution)/shard_map/all_gather | solution.py:371
  9.4 225.6 %all-gather.18.cloned.1.call-start = ((), (), s32[]{:S(2)}) async-start(), calls=%async_computation.14 | async-start | bytes 1216512 | tf_op jit(solution)/shard_map/all_gather | solution.py:372
  10.0 280.6 %all-gather.20.cloned.1.call-start = ((), (), s32[]{:S(2)}) async-start(), calls=%async_computation.15 | async-start | bytes 1216512 | tf_op jit(solution)/shard_map/all_gather | solution.py:373
  10.6 335.7 %all-gather.22.cloned.1.call-start = ((), (), s32[]{:S(2)}) async-start(), calls=%async_computation.16 | async-start | bytes 1216512 | tf_op jit(solution)/shard_map/all_gather | solution.py:374
  11.2 390.8 %all-gather.24.cloned.1.call-start = ((), (), s32[]{:S(2)}) async-start(), calls=%async_computation.17 | async-start | bytes 1216512 | tf_op jit(solution)/shard_map/all_gather | solution.py:375
  11.9 445.8 %all-gather.26.cloned.1.call-start = ((), (), s32[]{:S(2)}) async-start(), calls=%async_computation.18 | async-start | bytes 1216512 | tf_op jit(solution)/shard_map/all_gather | solution.py:376
  12.7 506.0 %all-gather.28.cloned.1.call-start = ((), (), s32[]{:S(2)}) async-start(), calls=%async_computation.19 | async-start | bytes 3244032 | tf_op jit(solution)/shard_map/all_gather | solution.py:382
  13.4 565.8 %all-gather.30.cloned.1.call-start = ((), (), s32[]{:S(2)}) async-start(), calls=%async_computation.20 | async-start | bytes 3244032 | tf_op jit(solution)/shard_map/all_gather | solution.py:383
  14.0 625.9 %all-gather.32.cloned.1.call-start = ((), (), s32[]{:S(2)}) async-start(), calls=%async_computation.21 | async-start | bytes 3244032 | tf_op jit(solution)/shard_map/all_gather | solution.py:384
  14.7 873.7 %reduce-scatter.24.cloned.1.call-start = ((), (), s32[]{:S(2)}) async-start(), calls=%async_computation.26 | async-start | bytes 2433024 | tf_op jit(solution)/shard_map/reduce_scatter | solution.py:413
  60.6 0.8 copy-start.44
  63.4 60.1 %copy-start.2 = (bf16[128,768]{1,0:T(8,128)(2,1)S(1)}, bf16[128,768]{1,0:T(8,128)(2,1)}, u32[]{:S(2)}) copy-start(bf16[128,768]{1,0:T(8,128)(2,1)} %param.29) | copy-start | bytes 589828
  196.1 39.0 %copy-start.28 = (bf16[12,128,64]{2,1,0:T(8,128)(2,1)}, bf16[12,128,64]{2,1,0:T(8,128)(2,1)S(1)}, u32[]{:S(2)}) copy-start(bf16[12,128,64]{2,1,0:T(8,128)(2,1)S(1)} %get-tuple-element.1146) | copy-start | bytes 589828
  196.1 39.0 %copy-start.29 = (bf16[12,128,64]{2,1,0:T(8,128)(2,1)}, bf16[12,128,64]{2,1,0:T(8,128)(2,1)S(1)}, u32[]{:S(2)}) copy-start(bf16[12,128,64]{2,1,0:T(8,128)(2,1)S(1)} %get-tuple-element.1147) | copy-start | bytes 589828
  196.1 96.2 %copy-start.30 = (bf16[12,128,64]{2,1,0:T(8,128)(2,1)}, bf16[12,128,64]{2,1,0:T(8,128)(2,1)S(1)}, u32[]{:S(2)}) copy-start(bf16[12,128,64]{2,1,0:T(8,128)(2,1)S(1)} %get-tuple-element.1148) | copy-start | bytes 589828
  196.1 96.2 %copy-start.40 = (f32[12,128]{1,0:T(8,128)}, f32[12,128]{1,0:T(8,128)S(1)}, u32[]{:S(2)}) copy-start(f32[12,128]{1,0:T(8,128)S(1)} %get-tuple-element.1177) | copy-start | bytes 18436
  196.1 96.2 %copy-start.41 = (f32[12,128]{1,0:T(8,128)}, f32[12,128]{1,0:T(8,128)S(1)}, u32[]{:S(2)}) copy-start(f32[12,128]{1,0:T(8,128)S(1)} %get-tuple-element.1050) | copy-start | bytes 18436
  409.8 48.0 %copy-start.31 = (bf16[12,128,64]{2,1,0:T(8,128)(2,1)}, bf16[12,128,64]{2,1,0:T(8,128)(2,1)S(1)}, u32[]{:S(2)}) copy-start(bf16[12,128,64]{2,1,0:T(8,128)(2,1)S(1)} %get-tuple-element.1149) | copy-start | bytes 589828
  409.8 49.8 %copy-start.36 = (bf16[12,64,64]{2,1,0:T(8,128)(2,1)}, bf16[12,64,64]{2,1,0:T(8,128)(2,1)S(1)}, u32[]{:S(2)}) copy-start(bf16[12,64,64]{2,1,0:T(8,128)(2,1)S(1)} %get-tuple-element.1151) | copy-start | bytes 294916
  459.6 119.6 %copy-start.5 = (bf16[128,768]{1,0:T(8,128)(2,1)}, bf16[128,768]{1,0:T(8,128)(2,1)S(1)}, u32[]{:S(2)}) copy-start(bf16[128,768]{1,0:T(8,128)(2,1)S(1)} %multiply_convert_fusion.2) | copy-start | bytes 589828
  522.1 117.8 %copy-start.34 = (bf16[128,768]{1,0:T(8,128)(2,1)S(1)}, bf16[128,768]{1,0:T(8,128)(2,1)}, u32[]{:S(2)}) copy-start(bf16[128,768]{1,0:T(8,128)(2,1)} %param.31) | copy-start | bytes 589828
  639.9 5.0 copy-start.3
  644.8 1.2 copy-start.22
  644.9 1.2 copy-start.20
  644.9 2.3 copy-start.4
  648.9 1.3 copy-start.16
  708.4 203.4 %reduce-scatter.26.cloned.1.call-start = ((), (), s32[]{:S(2)}) async-start(), calls=%async_computation.27 | async-start | bytes 2433024 | tf_op jit(solution)/shard_map/reduce_scatter | solution.py:416
  710.4 1.3 copy-start.17
  710.4 305.7 %reduce-scatter.22.cloned.1.call-start = ((), (), s32[]{:S(2)}) async-start(), calls=%async_computation.25 | async-start | bytes 2433024 | tf_op jit(solution)/shard_map/reduce_scatter | solution.py:412
  715.1 0.9 copy-start.37
  715.1 405.4 %reduce-scatter.34.cloned.1.call-start = ((), (), s32[]{:S(2)}) async-start(), calls=%async_computation.31 | async-start | bytes 2433024
  718.8 1.0 copy-start.8
  718.8 1.4 copy-start.15
  718.8 2.8 copy-start.38
  718.8 505.9 %reduce-scatter.36.cloned.1.call-start = ((), (), s32[]{:S(2)}) async-start(), calls=%async_computation.32 | async-start | bytes 2433024
  724.5 604.6 %reduce-scatter.16.cloned.1.call-start = ((), (), s32[]{:S(2)}) async-start(), calls=%async_computation.22 | async-start | bytes 2433024 | tf_op jit(solution)/shard_map/reduce_scatter | solution.py:409
  818.2 2.0 copy-start.42
  818.2 2.1 copy-start.24
  818.2 4.1 copy-start.26
  820.2 613.4 %reduce-scatter.18.cloned.1.call-start = ((), (), s32[]{:S(2)}) async-start(), calls=%async_computation.23 | async-start | bytes 2433024 | tf_op jit(solution)/shard_map/reduce_scatter | solution.py:410
  822.3 715.8 %reduce-scatter.20.cloned.1.call-start = ((), (), s32[]{:S(2)}) async-start(), calls=%async_computation.24 | async-start | bytes 2433024 | tf_op jit(solution)/shard_map/reduce_scatter | solution.py:411
  824.3 0.9 copy-start.6
  824.3 1.2 copy-start.23
  824.3 833.9 %reduce-scatter.28.cloned.1.call-start = ((), (), s32[]{:S(2)}) async-start(), calls=%async_computation.28 | async-start | bytes 6488064 | tf_op jit(solution)/shard_map/reduce_scatter | solution.py:401
  829.1 1.0 copy-start.21
  829.1 949.2 %reduce-scatter.30.cloned.1.call-start = ((), (), s32[]{:S(2)}) async-start(), calls=%async_computation.29 | async-start | bytes 6488064 | tf_op jit(solution)/shard_map/reduce_scatter | solution.py:402
  833.7 1.1 copy-start.18
  833.7 1.1 copy-start.35
  833.8 1064.7 %reduce-scatter.32.cloned.1.call-start = ((), (), s32[]{:S(2)}) async-start(), calls=%async_computation.30 | async-start | bytes 6488064 | tf_op jit(solution)/shard_map/reduce_scatter | solution.py:403
  838.5 1.3 copy-start.11
  838.5 1.8 copy-start.13
  838.5 1.8 copy-start.25
  840.3 1.3 copy-start.14
  840.3 1.3 copy-start.27
  841.6 41.0 %copy-start.45 = (f32[128]{0:T(128)S(1)}, f32[128]{0:T(128)}, u32[]{:S(2)}) copy-start(f32[128]{0:T(128)} %copy-done.44) | copy-start | bytes 1540
  841.6 41.0 %copy-start.9 = (f32[128,768]{1,0:T(8,128)S(1)}, f32[128,768]{1,0:T(8,128)}, u32[]{:S(2)}) copy-start(f32[128,768]{1,0:T(8,128)} %copy-done.7) | copy-start | bytes 1179652
  842.3 41.3 %copy-start.10 = (bf16[768,768]{1,0:T(8,128)(2,1)S(1)}, bf16[768,768]{1,0:T(8,128)(2,1)}, u32[]{:S(2)}) copy-start(bf16[768,768]{1,0:T(8,128)(2,1)} %all-gather.22.cloned.1.call-done) | copy-start | bytes 3538948
  882.6 1.4 copy-start.12
  882.6 1.4 copy-start.33
  884.0 1.2 copy-start.19
  884.1 1014.4 %copy-start.1 = (bf16[64,768]{1,0:T(8,128)(2,1)S(1)}, bf16[64,768]{1,0:T(8,128)(2,1)}, u32[]{:S(2)}) copy-start(bf16[64,768]{1,0:T(8,128)(2,1)} %param.30) | copy-start | bytes 294916
  (5 other events, 3.5 us)
Sparse Core Ops, SparseCore 0:
  10.9 56.9 all-gather.11
  70.8 52.7 all-gather.13
  126.4 52.8 all-gather.15
  182.0 52.9 all-gather.17
  237.8 52.8 all-gather.19
  293.4 52.8 all-gather.21
  349.1 52.8 all-gather.23
  404.9 52.8 all-gather.25
  460.6 57.9 all-gather.27
  521.3 57.8 all-gather.29
  582.0 57.8 all-gather.31
  708.5 98.5 reduce-scatter.23
  813.0 98.8 reduce-scatter.25
  917.6 98.5 reduce-scatter.21
  1021.8 98.6 reduce-scatter.33
  1126.3 98.4 reduce-scatter.35
  1230.4 98.6 reduce-scatter.15
  1334.9 98.6 reduce-scatter.17
  1439.4 98.6 reduce-scatter.19
  1544.1 114.0 reduce-scatter.27
  1664.4 113.8 reduce-scatter.29
  1784.6 113.8 reduce-scatter.31
where the time goes:
time: 1910 us
  waiting for transfers between devices  1550 us (81%)
  matrix products  178 us (9%)
  blocking collectives  80.8 us (4%)
  local copies, waits for them, and re-layouts  69.3 us (4%)
    unnamed x24, waiting for transfers between devices  216 us
    dot_general x201, matrix products, matmul(): return jnp.dot(left, right, preferred_element_type=jnp.float32)  176 us
    reduce_scatter x1, waiting for transfers between devices, body(): lax.psum_scatter(feed_grads[0], 'dp', scatter_dimension=0, tiled=True)  120 us
    reduce_scatter x1, waiting for transfers between devices, body(): lax.psum_scatter(feed_grads[1], 'dp', scatter_dimension=0, tiled=True)  120 us
    reduce_scatter x1, waiting for transfers between devices, body(): lax.psum_scatter(feed_grads[2], 'dp', scatter_dimension=0, tiled=True)  120 us
    reduce_scatter x1, waiting for transfers between devices, body(): lax.psum_scatter(matrices[2], 'dp', scatter_dimension=0, tiled=True)  105 us
    reduce_scatter x1, waiting for transfers between devices, body(): lax.psum_scatter(matrices[0], 'dp', scatter_dimension=0, tiled=True)  104 us
    reduce_scatter x1, waiting for transfers between devices, body(): lax.psum_scatter(matrices[1], 'dp', scatter_dimension=0, tiled=True)  104 us
  transfers between devices with their start and end apart: 22, of which 21 were waited for; matrix products, arithmetic and copies ran while one was open for 9% of the time, Pallas kernels for 0%

commit v1 on v0

v1 whole, which is shorter than its diff:
```python
import jax
import jax.numpy as jnp
from jax import lax
from jax.sharding import PartitionSpec as P

H = 12
AXIS = "dp"
EPSILON = 1e-06
MASKED = -1e30
BF = jnp.bfloat16
F32 = jnp.float32


def matmul(left, right):
    return jnp.dot(left, right, preferred_element_type=F32)


def matmul_nt(left, right):
    return lax.dot_general(left, right, (((1,), (1,)), ((), ())), preferred_element_type=F32)


def matmul_tn(left, right):
    return lax.dot_general(left, right, (((0,), (0,)), ((), ())), preferred_element_type=F32)


def bit_orders(count):
    bits = count.bit_length() - 1
    assert 1 << bits == count
    first = list(range(bits - 1, -1, -1))
    second = [{1: 2, 2: 1}.get(b, b) if bits > 2 else b for b in first]
    return first, second


def partner(count, bit):
    return [(i, i ^ (1 << bit)) for i in range(count)]


def own_bit(bit):
    return (lax.axis_index(AXIS) >> bit) & 1


def gather(piece, order, count):
    rows, columns = piece.shape
    held, done = piece[None], []
    for bit in order:
        other = lax.ppermute(held, AXIS, partner(count, bit))
        low = 1 << sum(1 for b in done if b < bit)
        shape = (held.shape[0] // low, 1, low, rows, columns)
        mine, theirs = held.reshape(shape), other.reshape(shape)
        upper = own_bit(bit) == 1
        held = jnp.concatenate(
            [jnp.where(upper, theirs, mine), jnp.where(upper, mine, theirs)], axis=1
        ).reshape(-1, rows, columns)
        done.append(bit)
    return held.reshape(count * rows, columns)


def scatter_sum(terms, order, count):
    rows, columns = terms.shape[0] // count, terms.shape[1]
    held = terms.astype(BF).reshape(count, rows, columns)
    left = list(range(count.bit_length() - 1))
    for step, bit in enumerate(order):
        low = 1 << sum(1 for b in left if b < bit)
        view = held.reshape(held.shape[0] // (2 * low), 2, low, rows, columns)
        mine = own_bit(bit)
        sent = lax.dynamic_index_in_dim(view, 1 - mine, 1, keepdims=False)
        kept = lax.dynamic_index_in_dim(view, mine, 1, keepdims=False)
        got = lax.ppermute(sent, AXIS, partner(count, bit))
        total = kept.astype(F32) + got.astype(F32)
        held = (total if step == len(order) - 1 else total.astype(BF)).reshape(-1, rows, columns)
        left.remove(bit)
    return held[0]


def total_sum(values, count):
    for bit in range(count.bit_length() - 1):
        values = values + lax.ppermute(values, AXIS, partner(count, bit))
    return values


def norm_scale_of(hidden):
    return lax.rsqrt(jnp.mean(hidden * hidden, axis=-1, keepdims=True) + EPSILON)


def norm_backward(hidden, scale, gain, cotangent):
    weighted = gain * cotangent
    grad_gain = jnp.sum(cotangent * hidden * scale, axis=0)
    inner = jnp.mean(weighted * hidden, axis=-1, keepdims=True)
    return scale * weighted - hidden * (scale * scale * scale) * inner, grad_gain


def toeplitz(vector):
    length = vector.shape[0]
    padded = jnp.concatenate([vector[::-1], jnp.zeros((length,), vector.dtype)])
    flattened = jnp.tile(padded, length + 1)[length - 1 : length - 1 + length * (2 * length - 1)]
    return flattened.reshape(length, 2 * length - 1)[:, :length]


def segment_ids(lengths, row_total):
    boundary = jnp.cumsum(lengths)
    row_index = jnp.arange(row_total, dtype=jnp.int32)
    return jnp.sum((row_index[:, None] >= boundary[None, :]).astype(jnp.int32), axis=1)


def heads_first(matrix):
    return matrix.reshape(matrix.shape[0], H, -1).transpose(1, 0, 2)


def heads_last(tensor):
    return tensor.transpose(1, 0, 2).reshape(tensor.shape[1], -1)


def batched(left, right, left_dim, right_dim):
    return lax.dot_general(
        left, right, (((left_dim,), (right_dim,)), ((0,), (0,))), preferred_element_type=F32
    )


def attend(query, key, value, bias, allowed):
    scores = batched(query, key, 2, 2)
    if bias is not None:
        scores = scores + bias
    scores = jnp.where(allowed[None], scores, MASKED)
    highest = jnp.max(scores, axis=2, keepdims=True)
    log_total = highest + jnp.log(jnp.sum(jnp.exp(scores - highest), axis=2, keepdims=True))
    weights = jnp.where(allowed[None], jnp.exp(scores - log_total), 0.0)
    mixed = batched(weights.astype(BF), value, 2, 1).astype(BF)
    return mixed, weights


def attend_backward(query, key, value, mixed, grad, weights):
    grad_weights = batched(grad, value, 2, 2)
    row_dot = jnp.sum(grad.astype(F32) * mixed.astype(F32), axis=2, keepdims=True)
    grad_scores = weights * (grad_weights - row_dot)
    low = grad_scores.astype(BF)
    grad_query = batched(low, key, 2, 1).astype(BF)
    grad_key = batched(low, query, 1, 1).astype(BF)
    grad_value = batched(weights.astype(BF), grad, 1, 1).astype(BF)
    return grad_query, grad_key, grad_value, grad_scores


def body(
    layer_input, encoder_states, output_grad,
    self_query, self_key, self_value, self_output,
    cross_query, cross_key, cross_value, cross_output,
    feed_gate, feed_up, feed_down,
    gain_self, gain_cross, gain_feed,
    bias_table, target_lengths, source_lengths, distance_bucket, *, count,
):
    order_a, order_b = bit_orders(count)
    width = layer_input.shape[1]
    rows = gain_self.shape[0]
    gains = jnp.stack([gain_self, gain_cross, gain_feed], axis=1)
    gains = jnp.pad(gains, ((0, 0), (0, 128 - gains.shape[1])))
    self_a = gather(jnp.concatenate([self_query, self_key, gains], axis=1), order_a, count)
    self_b = gather(jnp.concatenate([self_value, self_output], axis=1), order_b, count)
    cross_a = gather(jnp.concatenate([cross_key, cross_value], axis=1), order_a, count)
    cross_b = gather(jnp.concatenate([cross_query, cross_output], axis=1), order_b, count)
    gate = gather(feed_gate, order_a, count)
    up = gather(feed_up, order_b, count)
    half = feed_down.shape[1] // 2
    down_a = gather(feed_down[:, :half], order_a, count)
    down_b = gather(feed_down[:, half:], order_b, count)

    row_count = layer_input.shape[0]
    onehot = (
        distance_bucket[:, None] == jnp.arange(bias_table.shape[0], dtype=jnp.int32)[None, :]
    ).astype(F32)
    per_distance = jnp.dot(onehot, bias_table, precision=lax.Precision.HIGHEST)
    bias_rows = jnp.pad(per_distance.T, ((0, 0), (0, row_count - per_distance.shape[0])))
    bias, bias_pull = jax.vjp(jax.vmap(toeplitz), bias_rows)
    target_segment = segment_ids(target_lengths[0], row_count)
    source_segment = segment_ids(source_lengths[0], encoder_states.shape[0])
    position = jnp.arange(row_count, dtype=jnp.int32)
    causal = (target_segment[:, None] == target_segment[None, :]) & (
        position[None, :] <= position[:, None]
    )
    aligned = target_segment[:, None] == source_segment[None, :]

    gain_rows = self_a[:, 2 * width : 2 * width + 3].astype(F32).T
    gain_one, gain_two, gain_three = gain_rows[0:1], gain_rows[1:2], gain_rows[2:3]
    weight_v, weight_o = self_b[:, :width], self_b[:, width:]
    weight_qk = self_a[:, : 2 * width]
    weight_cq, weight_co = cross_b[:, :width], cross_b[:, width:]

    resid_zero = layer_input.astype(F32)
    scale_one = norm_scale_of(resid_zero)
    normed_one = (resid_zero * scale_one * gain_one).astype(BF)
    query_key = matmul(normed_one, weight_qk).astype(BF)
    value_rows = matmul(normed_one, weight_v).astype(BF)
    query_h, key_h = heads_first(query_key[:, :width]), heads_first(query_key[:, width:])
    value_h = heads_first(value_rows)
    mixed_one_h, weights_one = attend(query_h, key_h, value_h, bias, causal)
    mixed_one = heads_last(mixed_one_h)
    resid_one = resid_zero + matmul(mixed_one, weight_o)
    scale_two = norm_scale_of(resid_one)
    normed_two = (resid_one * scale_two * gain_two).astype(BF)
    cross_rows_h = heads_first(matmul(normed_two, weight_cq).astype(BF))
    cross_kv = matmul(encoder_states, cross_a).astype(BF)
    cross_keys_h, cross_values_h = heads_first(cross_kv[:, :width]), heads_first(cross_kv[:, width:])
    mixed_two_h, weights_two = attend(cross_rows_h, cross_keys_h, cross_values_h, None, aligned)
    mixed_two = heads_last(mixed_two_h)
    resid_two = resid_one + matmul(mixed_two, weight_co)
    scale_three = norm_scale_of(resid_two)
    normed_three = (resid_two * scale_three * gain_three).astype(BF)
    gate_part = matmul(normed_three, gate)
    linear_part = matmul(normed_three, up)
    hidden_f32, pullback = jax.vjp(
        lambda g, l: jax.nn.gelu(g, approximate=True) * l, gate_part, linear_part
    )
    hidden = hidden_f32.astype(BF)
    layer_output = jnp.concatenate(
        [
            resid_two[:, :half] + matmul(hidden, down_a),
            resid_two[:, half:] + matmul(hidden, down_b),
        ],
        axis=1,
    ).astype(BF)

    back_a, back_b = order_a[::-1], order_b[::-1]
    share_down_a = scatter_sum(matmul_tn(hidden, output_grad[:, :half]), back_a, count)
    share_down_b = scatter_sum(matmul_tn(hidden, output_grad[:, half:]), back_b, count)
    grad_hidden = matmul_nt(output_grad[:, :half], down_a) + matmul_nt(output_grad[:, half:], down_b)
    grad_gate, grad_linear = pullback(grad_hidden)
    grad_gate, grad_linear = grad_gate.astype(BF), grad_linear.astype(BF)
    share_gate = scatter_sum(matmul_tn(normed_three, grad_gate), back_a, count)
    share_up = scatter_sum(matmul_tn(normed_three, grad_linear), back_b, count)
    grad_normed = matmul_nt(grad_gate, gate) + matmul_nt(grad_linear, up)
    part, grad_gain_feed = norm_backward(resid_two, scale_three, gain_three, grad_normed)
    grad_resid_two = output_grad.astype(F32) + part

    low_two = grad_resid_two.astype(BF)
    share_co = scatter_sum(matmul_tn(mixed_two, low_two), back_a, count)
    grad_mixed_two = heads_first(matmul_nt(low_two, weight_co).astype(BF))
    grad_cq, grad_ck, grad_cv, _ = attend_backward(
        cross_rows_h, cross_keys_h, cross_values_h, mixed_two_h, grad_mixed_two, weights_two
    )
    grad_cross_rows = heads_last(grad_cq)
    grad_cross_kv = jnp.concatenate([heads_last(grad_ck), heads_last(grad_cv)], axis=1)
    share_cq = scatter_sum(matmul_tn(normed_two, grad_cross_rows), back_b, count)
    terms_kv = matmul_tn(encoder_states, grad_cross_kv)
    share_ck = scatter_sum(terms_kv[:, :width], back_a, count)
    share_cv = scatter_sum(terms_kv[:, width:], back_b, count)
    encoder_grad = matmul_nt(grad_cross_kv, cross_a)
    part, grad_gain_cross = norm_backward(
        resid_one, scale_two, gain_two, matmul_nt(grad_cross_rows, weight_cq)
    )
    grad_resid_one = grad_resid_two + part

    low_one = grad_resid_one.astype(BF)
    share_o = scatter_sum(matmul_tn(mixed_one, low_one), back_a, count)
    grad_mixed_one = heads_first(matmul_nt(low_one, weight_o).astype(BF))
    grad_q, grad_k, grad_v, grad_scores = attend_backward(
        query_h, key_h, value_h, mixed_one_h, grad_mixed_one, weights_one
    )
    grad_qk = jnp.concatenate([heads_last(grad_q), heads_last(grad_k)], axis=1)
    grad_value_rows = heads_last(grad_v)
    share_v = scatter_sum(matmul_tn(normed_one, grad_value_rows), back_b, count)
    terms_qk = matmul_tn(normed_one, grad_qk)
    share_q = scatter_sum(terms_qk[:, :width], back_a, count)
    share_k = scatter_sum(terms_qk[:, width:], back_b, count)
    part, grad_gain_self = norm_backward(
        resid_zero, scale_one, gain_one,
        matmul_nt(grad_qk, weight_qk) + matmul_nt(grad_value_rows, weight_v),
    )
    input_grad = grad_resid_one + part
    grad_bias_rows = bias_pull(grad_scores)[0]
    grad_table = jnp.dot(
        onehot.T, grad_bias_rows[:, : onehot.shape[0]].T, precision=lax.Precision.HIGHEST
    )
    table_rows = jnp.pad(grad_table, ((0, 0), (0, width - grad_table.shape[1])))
    small = jnp.concatenate(
        [grad_gain_self[None], grad_gain_cross[None], grad_gain_feed[None], table_rows], axis=0
    )
    small = total_sum(small, count)
    own = lax.dynamic_slice_in_dim(small[:3], lax.axis_index(AXIS) * rows, rows, axis=1)
    return (
        layer_output, input_grad, encoder_grad,
        share_q, share_k, share_v, share_o,
        share_cq, share_ck, share_cv, share_co,
        share_gate, share_up, jnp.concatenate([share_down_a, share_down_b], axis=1),
        own[0], own[1], own[2], small[3:, : grad_table.shape[1]],
    )


def solution(mesh):
    count = mesh.shape[AXIS]
    rows, flat, full = P(AXIS, None), P(AXIS), P()

    def step(*args):
        return body(*args, count=count)

    return jax.shard_map(
        step,
        mesh=mesh,
        in_specs=(rows,) * 14 + (flat,) * 3 + (full, rows, rows, full),
        out_specs=(rows,) * 14 + (flat,) * 3 + (full,),
        check_vma=False,
    )
```

time: 1910 us -> 523 us (0.27)
  waiting for transfers between devices: 1550 us -> 227 us
  matrix products: 178 us -> 60.1 us
  starting transfers between devices: 1.05 us -> 113 us
  blocking collectives: 80.8 us -> 0 us
  other arithmetic: 8.62 us -> 45.7 us
    reduce_scatter x9 -> x0, waiting for transfers between devices: 801 us -> none  [the longest x1 120 us: body(): lax.psum_scatter(feed_grads[0], 'dp', scatter_dimension=0, tiled=True)]
    all_gather x11 -> x0, waiting for transfers between devices: 533 us -> none  [the longest x1 59 us: body(): lax.all_gather(feed_gate, 'dp', axis=0, tiled=True)]
    ppermute x0 -> x105, waiting for transfers between devices: none -> 227 us  [the longest x60 146 us: scatter_sum(): got = lax.ppermute(sent, AXIS, partner(count, bit))]
    unnamed x24 -> x0, waiting for transfers between devices: 216 us -> none
    dot_general x203 -> x43, matrix products: 178 us -> 59.8 us  [the longest x10 18.4 us: matmul_tn(): lax.dot_general(left, right, (((0,), (0,)), ((), ())), preferred_element_...]
    ppermute x0 -> x105, starting transfers between devices: none -> 113 us  [the longest x60 60.1 us: scatter_sum(): got = lax.ppermute(sent, AXIS, partner(count, bit))]
    unnamed x1 -> x0, blocking collectives: 42.2 us -> none
    psum x1 -> x0, blocking collectives: 38.5 us -> none  [body(): lax.psum((table_grad(onehot, grad_bias_rows), grad_gain_self, grad_gain_c...]
  transfers between devices with their start and end apart: 22 -> 105, of which waited for: 21 -> 59; matrix products, arithmetic and copies ran while one was open for 9% -> 18% of each run, Pallas kernels for 0% -> 0%
where the time goes in v1:
time: 523 us; the launch traced here: 513 us
  waiting for transfers between devices  227 us (43%)
  starting transfers between devices  113 us (22%)
  local copies, waits for them, and re-layouts  63 us (12%)
  matrix products  60.1 us (11%)
  other arithmetic  45.7 us (9%)
    ppermute x60, waiting for transfers between devices, scatter_sum(): got = lax.ppermute(sent, AXIS, partner(count, bit))  146 us
    ppermute x40, waiting for transfers between devices, gather(): other = lax.ppermute(held, AXIS, partner(count, bit))  71.3 us
    ppermute x60, starting transfers between devices, scatter_sum(): got = lax.ppermute(sent, AXIS, partner(count, bit))  60.1 us
    ppermute x40, starting transfers between devices, gather(): other = lax.ppermute(held, AXIS, partner(count, bit))  42 us
    dot_general x10, matrix products, matmul_tn(): lax.dot_general(left, right, (((0,), (0,)), ((), ())), preferred_element_...  18.4 us
    dot_general x12, matrix products, batched(): lax.dot_general(left, right, (((left_dim,), (right_dim,)), ((0,), (0,))),...  16.2 us
    unnamed x200, local copies, waits for them, and re-layouts  15.6 us
    dot_general x10, matrix products, matmul_nt(): lax.dot_general(left, right, (((1,), (1,)), ((), ())), preferred_element_...  13.2 us
  transfers between devices with their start and end apart: 105, of which 59 were waited for; matrix products, arithmetic and copies ran while one was open for 18% of the time, Pallas kernels for 0%

profile of v1, /device:TPU:0, one launch (start us, length us, event | category | flops | bytes accessed | tf_op | source)
XLA Modules:
  0.0 513.0 jit_solution(7619347572373796129)
XLA Ops:
  0.7 4.1 collective-permute-start.20
  5.7 2.8 collective-permute-start.10
  10.2 2.8 collective-permute-start.30
  21.6 3.4 reshape.1697
  27.6 2.9 collective-permute-start.5
  30.7 6.8 %collective-permute-done.5 = bf16[1,24,1536]{2,1,0:T(8,128)(2,1)S(1)} collective-permute-done((bf16[1,24,1536]{2,1,0:T(8,128)(2,1)S(1)}, bf16[1,24,1536]{2,1,0:T(8,128)(2,1)S(1)}, u32[]{:S(2)}, u32[]{:S(2)}) %collective-permute-start.5) | collective-permute-done | bytes 73760 | tf_op jit(solution)/shard_map/ppermute | solution.py:46
  44.3 11.2 %collective-permute-done.36 = bf16[2,64,384]{2,1,0:T(8,128)(2,1)S(1)} collective-permute-done((bf16[2,64,384]{2,1,0:T(8,128)(2,1)S(1)}, bf16[2,64,384]{2,1,0:T(8,128)(2,1)S(1)}, u32[]{:S(2)}, u32[]{:S(2)}) %collective-permute-start.36) | collective-permute-done | bytes 98336 | tf_op jit(solution)/shard_map/ppermute | solution.py:46
  69.4 4.2 collective-permute-done.12
  75.2 4.8 collective-permute-done.7
  84.3 6.1 %collective-permute-done.22 = bf16[4,24,2048]{2,1,0:T(8,128)(2,1)S(1)} collective-permute-done((bf16[4,24,2048]{2,1,0:T(8,128)(2,1)S(1)}, bf16[4,24,2048]{2,1,0:T(8,128)(2,1)S(1)}, u32[]{:S(2)}, u32[]{:S(2)}) %collective-permute-start.22) | collective-permute-done | bytes 393248 | tf_op jit(solution)/shard_map/ppermute | solution.py:46
  93.0 3.8 collective-permute-done.33
  99.7 11.8 %collective-permute-done.13 = bf16[8,24,1536]{2,1,0:T(8,128)(2,1)S(1)} collective-permute-done((bf16[8,24,1536]{2,1,0:T(8,128)(2,1)S(1)}, bf16[8,24,1536]{2,1,0:T(8,128)(2,1)S(1)}, u32[]{:S(2)}, u32[]{:S(2)}) %collective-permute-start.13) | collective-permute-done | bytes 589856 | tf_op jit(solution)/shard_map/ppermute | solution.py:46
  113.3 10.8 %collective-permute-done.8 = bf16[8,24,1536]{2,1,0:T(8,128)(2,1)S(1)} collective-permute-done((bf16[8,24,1536]{2,1,0:T(8,128)(2,1)S(1)}, bf16[8,24,1536]{2,1,0:T(8,128)(2,1)S(1)}, u32[]{:S(2)}, u32[]{:S(2)}) %collective-permute-start.8) | collective-permute-done | bytes 589856 | tf_op jit(solution)/shard_map/ppermute | solution.py:46
  127.0 8.0 %collective-permute-done.23 = bf16[8,24,2048]{2,1,0:T(8,128)(2,1)S(1)} collective-permute-done((bf16[8,24,2048]{2,1,0:T(8,128)(2,1)S(1)}, bf16[8,24,2048]{2,1,0:T(8,128)(2,1)S(1)}, u32[]{:S(2)}, u32[]{:S(2)}) %collective-permute-start.23) | collective-permute-done | bytes 786464 | tf_op jit(solution)/shard_map/ppermute | solution.py:46
  181.7 2.3 fusion.37
  201.4 2.2 fusion.12
  203.7 2.3 copy.476
  206.0 2.3 convolution_convert_fusion.12
  214.2 2.7 convolution_convert_fusion.2
  216.9 2.7 convolution_convert_fusion.3
  229.1 2.2 fusion.2
  235.7 2.5 reshape.1753
  262.4 3.4 collective-permute-done.101
  268.3 2.4 collective-permute-done.102
  275.8 5.9 %collective-permute-start.104 = (f32[35,768]{1,0:T(8,128)S(1)}, f32[35,768]{1,0:T(8,128)S(1)}, u32[]{:S(2)}, u32[]{:S(2)}) collective-permute-start(f32[35,768]{1,0:T(8,128)S(1)} %add.557), channel_id=1, source_target_pairs={{0,16},{1,17},{2,18},{3,19},{4,20},{5,21},{6,22},{7,23},{8,24},{9,... | collective-permute-start | bytes 322568 | tf_op jit(solution)/shard_map/ppermute | solution.py:77
  282.3 2.5 collective-permute-done.104
  294.4 4.6 collective-permute-done.40
  305.8 3.1 collective-permute-done.76
  311.2 4.0 collective-permute-done.66
  317.9 2.8 collective-permute-done.56
  321.2 3.9 collective-permute-done.51
  325.6 3.3 collective-permute-done.46
  332.2 8.4 %collective-permute-done.77 = bf16[4,1,24,768]{3,2,0,1:T(8,128)(2,1)S(1)} collective-permute-done((bf16[4,1,24,768]{3,2,0,1:T(8,128)(2,1)S(1)}, bf16[4,1,24,768]{3,2,0,1:T(8,128)(2,1)S(1)}, u32[]{:S(2)}, u32[]{:S(2)}) %collective-permute-start.77) | collective-permute-done | bytes 147488 | tf_op jit(solution)/shard_map/ppermute | solution.py:68
  341.1 4.7 collective-permute-done.72
  347.4 3.6 collective-permute-done.67
  351.4 4.7 collective-permute-done.62
  357.7 3.6 collective-permute-done.57
  361.7 4.7 collective-permute-done.52
  366.8 4.7 collective-permute-done.47
  373.1 3.5 collective-permute-done.42
  376.7 4.3 collective-permute-done.78
  381.1 4.5 collective-permute-done.73
  385.6 4.5 collective-permute-done.68
  390.5 4.0 collective-permute-done.63
  394.8 4.0 collective-permute-done.58
  399.3 3.9 collective-permute-done.53
  403.7 3.9 collective-permute-done.48
  408.1 3.9 collective-permute-done.43
  411.9 3.2 collective-permute-start.79
  417.3 2.7 collective-permute-start.74
  422.2 2.8 collective-permute-start.69
  427.0 2.8 collective-permute-start.64
  431.9 2.8 collective-permute-start.59
  435.3 2.3 collective-permute-done.59
  440.3 2.2 collective-permute-done.54
  445.1 2.2 collective-permute-done.49
  450.0 2.2 collective-permute-done.44
  455.4 5.5 %collective-permute-done.92 = bf16[4,1,64,384]{3,2,0,1:T(8,128)(2,1)S(1)} collective-permute-done((bf16[4,1,64,384]{3,2,0,1:T(8,128)(2,1)S(1)}, bf16[4,1,64,384]{3,2,0,1:T(8,128)(2,1)S(1)}, u32[]{:S(2)}, u32[]{:S(2)}) %collective-permute-start.92) | collective-permute-done | bytes 196640 | tf_op jit(solution)/shard_map/ppermute | solution.py:68
  463.5 4.5 collective-permute-done.93
  471.2 3.8 collective-permute-done.94
  479.9 9.0 %collective-permute-done.86 = bf16[4,2,24,2048]{3,2,1,0:T(8,128)(2,1)S(1)} collective-permute-done((bf16[4,2,24,2048]{3,2,1,0:T(8,128)(2,1)S(1)}, bf16[4,2,24,2048]{3,2,1,0:T(8,128)(2,1)S(1)}, u32[]{:S(2)}, u32[]{:S(2)}) %collective-permute-start.86) | collective-permute-done | bytes 786464 | tf_op jit(solution)/shard_map/ppermute | solution.py:68
  492.1 5.0 collective-permute-done.87
  499.6 3.4 collective-permute-done.88
  506.8 3.0 collective-permute-done.89
  (696 shorter events, 242.2 us)
Async XLA Ops:
  0.7 39.1 %collective-permute-start.20 = (bf16[1,24,2048]{2,1,0:T(8,128)(2,1)}, bf16[1,24,2048]{2,1,0:T(8,128)(2,1)S(1)}, u32[]{:S(2)}, u32[]{:S(2)}) collective-permute-start(bf16[1,24,2048]{2,1,0:T(8,128)(2,1)} %bitcast.941), channel_id=1, source_target_pairs={{0,16},{1,17},{2,18},{3,19},{4,20},{5,21},{6,22},{7,23},{8,24},{9,... | collective-permute-start | bytes 294920 | tf_op jit(solution)/shard_map/ppermute | solution.py:46
  4.8 35.1 %collective-permute-start.25 = (bf16[1,24,2048]{2,1,0:T(8,128)(2,1)}, bf16[1,24,2048]{2,1,0:T(8,128)(2,1)S(1)}, u32[]{:S(2)}, u32[]{:S(2)}) collective-permute-start(bf16[1,24,2048]{2,1,0:T(8,128)(2,1)} %bitcast.940), channel_id=1, source_target_pairs={{0,16},{1,17},{2,18},{3,19},{4,20},{5,21},{6,22},{7,23},{8,24},{9,... | collective-permute-start | bytes 294920 | tf_op jit(solution)/shard_map/ppermute | solution.py:46
  5.7 21.9 %collective-permute-start.10 = (bf16[1,24,1536]{2,1,0:T(8,128)(2,1)S(1)}, bf16[1,24,1536]{2,1,0:T(8,128)(2,1)S(1)}, u32[]{:S(2)}, u32[]{:S(2)}) collective-permute-start(bf16[1,24,1536]{2,1,0:T(8,128)(2,1)S(1)} %maximum_bitcast_fusion.11), channel_id=1, source_target_pairs={{0,16},{1,17},{2,18},{3,19},{4,20},{5,21},{6,22},{7,23},{8,24},{9,... | collective-permute-start | bytes 221192 | tf_op jit(solution)/shard_map/ppermute | solution.py:46
  9.3 21.2 %collective-permute-start.15 = (bf16[1,24,1536]{2,1,0:T(8,128)(2,1)S(1)}, bf16[1,24,1536]{2,1,0:T(8,128)(2,1)S(1)}, u32[]{:S(2)}, u32[]{:S(2)}) collective-permute-start(bf16[1,24,1536]{2,1,0:T(8,128)(2,1)S(1)} %maximum_bitcast_fusion.10), channel_id=1, source_target_pairs={{0,16},{1,17},{2,18},{3,19},{4,20},{5,21},{6,22},{7,23},{8,24},{9,... | collective-permute-start | bytes 221192 | tf_op jit(solution)/shard_map/ppermute | solution.py:46
  10.2 17.2 %collective-permute-start.30 = (bf16[1,64,384]{2,1,0:T(8,128)(2,1)S(1)}, bf16[1,64,384]{2,1,0:T(8,128)(2,1)S(1)}, u32[]{:S(2)}, u32[]{:S(2)}) collective-permute-start(bf16[1,64,384]{2,1,0:T(8,128)(2,1)S(1)} %slice_bitcast_fusion.1), channel_id=1, source_target_pairs={{0,16},{1,17},{2,18},{3,19},{4,20},{5,21},{6,22},{7,23},{8,24},{9,... | collective-permute-start | bytes 147464 | tf_op jit(solution)/shard_map/ppermute | solution.py:46
  27.4 10.2 %collective-permute-start = (bf16[1,24,1664]{2,1,0:T(8,128)(2,1)S(1)}, bf16[1,24,1664]{2,1,0:T(8,128)(2,1)S(1)}, u32[]{:S(2)}, u32[]{:S(2)}) collective-permute-start(bf16[1,24,1664]{2,1,0:T(8,128)(2,1)S(1)} %maximum_bitcast_fusion.8), channel_id=1, source_target_pairs={{0,16},{1,17},{2,18},{3,19},{4,20},{5,21},{6,22},{7,23},{8,24},{9,... | collective-permute-start | bytes 239624 | tf_op jit(solution)/shard_map/ppermute | solution.py:46
  27.6 10.0 %collective-permute-start.5 = (bf16[1,24,1536]{2,1,0:T(8,128)(2,1)S(1)}, bf16[1,24,1536]{2,1,0:T(8,128)(2,1)S(1)}, u32[]{:S(2)}, u32[]{:S(2)}) collective-permute-start(bf16[1,24,1536]{2,1,0:T(8,128)(2,1)S(1)} %maximum_bitcast_fusion.9), channel_id=1, source_target_pairs={{0,16},{1,17},{2,18},{3,19},{4,20},{5,21},{6,22},{7,23},{8,24},{9,... | collective-permute-start | bytes 221192 | tf_op jit(solution)/shard_map/ppermute | solution.py:46
  30.5 11.5 %collective-permute-start.35 = (bf16[1,64,384]{2,1,0:T(8,128)(2,1)S(1)}, bf16[1,64,384]{2,1,0:T(8,128)(2,1)S(1)}, u32[]{:S(2)}, u32[]{:S(2)}) collective-permute-start(bf16[1,64,384]{2,1,0:T(8,128)(2,1)S(1)} %get-tuple-element.154), channel_id=1, source_target_pairs={{0,16},{1,17},{2,18},{3,19},{4,20},{5,21},{6,22},{7,23},{8,24},{9,... | collective-permute-start | bytes 147464 | tf_op jit(solution)/shard_map/ppermute | solution.py:46
  37.6 18.5 %collective-permute-start.11 = (bf16[2,24,1536]{2,1,0:T(8,128)(2,1)S(1)}, bf16[2,24,1536]{2,1,0:T(8,128)(2,1)S(1)}, u32[]{:S(2)}, u32[]{:S(2)}) collective-permute-start(bf16[2,24,1536]{2,1,0:T(8,128)(2,1)S(1)} %maximum_bitcast_fusion.5), channel_id=1, source_target_pairs={{0,8},{1,9},{2,10},{3,11},{4,12},{5,13},{6,14},{7,15},{8,0},{9,1},... | collective-permute-start | bytes 442376 | tf_op jit(solution)/shard_map/ppermute | solution.py:46
  39.8 19.7 %collective-permute-start.6 = (bf16[2,24,1536]{2,1,0:T(8,128)(2,1)S(1)}, bf16[2,24,1536]{2,1,0:T(8,128)(2,1)S(1)}, u32[]{:S(2)}, u32[]{:S(2)}) collective-permute-start(bf16[2,24,1536]{2,1,0:T(8,128)(2,1)S(1)} %maximum_bitcast_fusion.3), channel_id=1, source_target_pairs={{0,8},{1,9},{2,10},{3,11},{4,12},{5,13},{6,14},{7,15},{8,0},{9,1},... | collective-permute-start | bytes 442376 | tf_op jit(solution)/shard_map/ppermute | solution.py:46
  39.9 17.9 %collective-permute-start.16 = (bf16[2,24,1536]{2,1,0:T(8,128)(2,1)S(1)}, bf16[2,24,1536]{2,1,0:T(8,128)(2,1)S(1)}, u32[]{:S(2)}, u32[]{:S(2)}) collective-permute-start(bf16[2,24,1536]{2,1,0:T(8,128)(2,1)S(1)} %maximum_bitcast_fusion.4), channel_id=1, source_target_pairs={{0,8},{1,9},{2,10},{3,11},{4,12},{5,13},{6,14},{7,15},{8,0},{9,1},... | collective-permute-start | bytes 442376 | tf_op jit(solution)/shard_map/ppermute | solution.py:46
  42.0 19.1 %collective-permute-start.1 = (bf16[2,24,1664]{2,1,0:T(8,128)(2,1)S(1)}, bf16[2,24,1664]{2,1,0:T(8,128)(2,1)S(1)}, u32[]{:S(2)}, u32[]{:S(2)}) collective-permute-start(bf16[2,24,1664]{2,1,0:T(8,128)(2,1)S(1)} %maximum_bitcast_fusion.2), channel_id=1, source_target_pairs={{0,8},{1,9},{2,10},{3,11},{4,12},{5,13},{6,14},{7,15},{8,0},{9,1},... | collective-permute-start | bytes 479240 | tf_op jit(solution)/shard_map/ppermute | solution.py:46
  43.2 12.3 %collective-permute-start.36 = (bf16[2,64,384]{2,1,0:T(8,128)(2,1)S(1)}, bf16[2,64,384]{2,1,0:T(8,128)(2,1)S(1)}, u32[]{:S(2)}, u32[]{:S(2)}) collective-permute-start(bf16[2,64,384]{2,1,0:T(8,128)(2,1)S(1)} %maximum_bitcast_fusion.7), channel_id=1, source_target_pairs={{0,8},{1,9},{2,10},{3,11},{4,12},{5,13},{6,14},{7,15},{8,0},{9,1},... | collective-permute-start | bytes 294920 | tf_op jit(solution)/shard_map/ppermute | solution.py:46
  55.5 9.7 %collective-permute-start.21 = (bf16[2,24,2048]{2,1,0:T(8,128)(2,1)S(1)}, bf16[2,24,2048]{2,1,0:T(8,128)(2,1)S(1)}, u32[]{:S(2)}, u32[]{:S(2)}) collective-permute-start(bf16[2,24,2048]{2,1,0:T(8,128)(2,1)S(1)} %maximum_bitcast_fusion), channel_id=1, source_target_pairs={{0,8},{1,9},{2,10},{3,11},{4,12},{5,13},{6,14},{7,15},{8,0},{9,1},... | collective-permute-start | bytes 589832 | tf_op jit(solution)/shard_map/ppermute | solution.py:46
  56.1 7.5 %collective-permute-start.26 = (bf16[2,24,2048]{2,1,0:T(8,128)(2,1)S(1)}, bf16[2,24,2048]{2,1,0:T(8,128)(2,1)S(1)}, u32[]{:S(2)}, u32[]{:S(2)}) collective-permute-start(bf16[2,24,2048]{2,1,0:T(8,128)(2,1)S(1)} %maximum_bitcast_fusion.1), channel_id=1, source_target_pairs={{0,8},{1,9},{2,10},{3,11},{4,12},{5,13},{6,14},{7,15},{8,0},{9,1},... | collective-permute-start | bytes 589832 | tf_op jit(solution)/shard_map/ppermute | solution.py:46
  57.8 9.1 %collective-permute-start.32 = (bf16[4,64,384]{2,1,0:T(8,128)(2,1)S(1)}, bf16[4,64,384]{2,1,0:T(8,128)(2,1)S(1)}, u32[]{:S(2)}, u32[]{:S(2)}) collective-permute-start(bf16[4,64,384]{2,1,0:T(8,128)(2,1)S(1)} %bitcast.901), channel_id=1, source_target_pairs={{0,4},{1,5},{2,6},{3,7},{4,0},{5,1},{6,2},{7,3},{8,12},{9,13},{10,... | collective-permute-start | bytes 589832 | tf_op jit(solution)/shard_map/ppermute | solution.py:46
  59.5 8.2 %collective-permute-start.37 = (bf16[4,64,384]{2,1,0:T(8,128)(2,1)S(1)}, bf16[4,64,384]{2,1,0:T(8,128)(2,1)S(1)}, u32[]{:S(2)}, u32[]{:S(2)}) collective-permute-start(bf16[4,64,384]{2,1,0:T(8,128)(2,1)S(1)} %bitcast.902), channel_id=1, source_target_pairs={{0,2},{1,3},{2,0},{3,1},{4,6},{5,7},{6,4},{7,5},{8,10},{9,11},{10,... | collective-permute-start | bytes 589832 | tf_op jit(solution)/shard_map/ppermute | solution.py:46
  61.1 12.5 %collective-permute-start.12 = (bf16[4,24,1536]{2,1,0:T(8,128)(2,1)S(1)}, bf16[4,24,1536]{2,1,0:T(8,128)(2,1)S(1)}, u32[]{:S(2)}, u32[]{:S(2)}) collective-permute-start(bf16[4,24,1536]{2,1,0:T(8,128)(2,1)S(1)} %bitcast.894), channel_id=1, source_target_pairs={{0,2},{1,3},{2,0},{3,1},{4,6},{5,7},{6,4},{7,5},{8,10},{9,11},{10,... | collective-permute-start | bytes 884744 | tf_op jit(solution)/shard_map/ppermute | solution.py:46
  63.6 16.4 %collective-permute-start.7 = (bf16[4,24,1536]{2,1,0:T(8,128)(2,1)S(1)}, bf16[4,24,1536]{2,1,0:T(8,128)(2,1)S(1)}, u32[]{:S(2)}, u32[]{:S(2)}) collective-permute-start(bf16[4,24,1536]{2,1,0:T(8,128)(2,1)S(1)} %bitcast.895), channel_id=1, source_target_pairs={{0,2},{1,3},{2,0},{3,1},{4,6},{5,7},{6,4},{7,5},{8,10},{9,11},{10,... | collective-permute-start | bytes 884744 | tf_op jit(solution)/shard_map/ppermute | solution.py:46
  65.2 16.4 %collective-permute-start.17 = (bf16[4,24,1536]{2,1,0:T(8,128)(2,1)S(1)}, bf16[4,24,1536]{2,1,0:T(8,128)(2,1)S(1)}, u32[]{:S(2)}, u32[]{:S(2)}) collective-permute-start(bf16[4,24,1536]{2,1,0:T(8,128)(2,1)S(1)} %bitcast.893), channel_id=1, source_target_pairs={{0,4},{1,5},{2,6},{3,7},{4,0},{5,1},{6,2},{7,3},{8,12},{9,13},{10,... | collective-permute-start | bytes 884744 | tf_op jit(solution)/shard_map/ppermute | solution.py:46
  66.9 15.6 %collective-permute-start.2 = (bf16[4,24,1664]{2,1,0:T(8,128)(2,1)S(1)}, bf16[4,24,1664]{2,1,0:T(8,128)(2,1)S(1)}, u32[]{:S(2)}, u32[]{:S(2)}) collective-permute-start(bf16[4,24,1664]{2,1,0:T(8,128)(2,1)S(1)} %bitcast.884), channel_id=1, source_target_pairs={{0,4},{1,5},{2,6},{3,7},{4,0},{5,1},{6,2},{7,3},{8,12},{9,13},{10,... | collective-permute-start | bytes 958472 | tf_op jit(solution)/shard_map/ppermute | solution.py:46
  67.7 22.8 %collective-permute-start.22 = (bf16[4,24,2048]{2,1,0:T(8,128)(2,1)S(1)}, bf16[4,24,2048]{2,1,0:T(8,128)(2,1)S(1)}, u32[]{:S(2)}, u32[]{:S(2)}) collective-permute-start(bf16[4,24,2048]{2,1,0:T(8,128)(2,1)S(1)} %bitcast.877), channel_id=1, source_target_pairs={{0,4},{1,5},{2,6},{3,7},{4,0},{5,1},{6,2},{7,3},{8,12},{9,13},{10,... | collective-permute-start | bytes 1179656 | tf_op jit(solution)/shard_map/ppermute | solution.py:46
  73.7 18.4 %collective-permute-start.27 = (bf16[4,24,2048]{2,1,0:T(8,128)(2,1)S(1)}, bf16[4,24,2048]{2,1,0:T(8,128)(2,1)S(1)}, u32[]{:S(2)}, u32[]{:S(2)}) collective-permute-start(bf16[4,24,2048]{2,1,0:T(8,128)(2,1)S(1)} %bitcast.875), channel_id=1, source_target_pairs={{0,2},{1,3},{2,0},{3,1},{4,6},{5,7},{6,4},{7,5},{8,10},{9,11},{10,... | collective-permute-start | bytes 1179656 | tf_op jit(solution)/shard_map/ppermute | solution.py:46
  80.0 16.9 %collective-permute-start.33 = (bf16[8,64,384]{2,1,0:T(8,128)(2,1)S(1)}, bf16[8,64,384]{2,1,0:T(8,128)(2,1)S(1)}, u32[]{:S(2)}, u32[]{:S(2)}) collective-permute-start(bf16[8,64,384]{2,1,0:T(8,128)(2,1)S(1)} %bitcast.876), channel_id=1, source_target_pairs={{0,2},{1,3},{2,0},{3,1},{4,6},{5,7},{6,4},{7,5},{8,10},{9,11},{10,... | collective-permute-start | bytes 1179656 | tf_op jit(solution)/shard_map/ppermute | solution.py:46
  81.6 17.3 %collective-permute-start.38 = (bf16[8,64,384]{2,1,0:T(8,128)(2,1)S(1)}, bf16[8,64,384]{2,1,0:T(8,128)(2,1)S(1)}, u32[]{:S(2)}, u32[]{:S(2)}) collective-permute-start(bf16[8,64,384]{2,1,0:T(8,128)(2,1)S(1)} %bitcast.930), channel_id=1, source_target_pairs={{0,4},{1,5},{2,6},{3,7},{4,0},{5,1},{6,2},{7,3},{8,12},{9,13},{10,... | collective-permute-start | bytes 1179656 | tf_op jit(solution)/shard_map/ppermute | solution.py:46
  82.5 29.0 %collective-permute-start.13 = (bf16[8,24,1536]{2,1,0:T(8,128)(2,1)S(1)}, bf16[8,24,1536]{2,1,0:T(8,128)(2,1)S(1)}, u32[]{:S(2)}, u32[]{:S(2)}) collective-permute-start(bf16[8,24,1536]{2,1,0:T(8,128)(2,1)S(1)} %bitcast.913), channel_id=1, source_target_pairs={{0,4},{1,5},{2,6},{3,7},{4,0},{5,1},{6,2},{7,3},{8,12},{9,13},{10,... | collective-permute-start | bytes 1769480 | tf_op jit(solution)/shard_map/ppermute | solution.py:46
  90.4 33.7 %collective-permute-start.8 = (bf16[8,24,1536]{2,1,0:T(8,128)(2,1)S(1)}, bf16[8,24,1536]{2,1,0:T(8,128)(2,1)S(1)}, u32[]{:S(2)}, u32[]{:S(2)}) collective-permute-start(bf16[8,24,1536]{2,1,0:T(8,128)(2,1)S(1)} %bitcast.912), channel_id=1, source_target_pairs={{0,4},{1,5},{2,6},{3,7},{4,0},{5,1},{6,2},{7,3},{8,12},{9,13},{10,... | collective-permute-start | bytes 1769480 | tf_op jit(solution)/shard_map/ppermute | solution.py:46
  92.1 32.4 %collective-permute-start.18 = (bf16[8,24,1536]{2,1,0:T(8,128)(2,1)S(1)}, bf16[8,24,1536]{2,1,0:T(8,128)(2,1)S(1)}, u32[]{:S(2)}, u32[]{:S(2)}) collective-permute-start(bf16[8,24,1536]{2,1,0:T(8,128)(2,1)S(1)} %bitcast.845), channel_id=1, source_target_pairs={{0,2},{1,3},{2,0},{3,1},{4,6},{5,7},{6,4},{7,5},{8,10},{9,11},{10,... | collective-permute-start | bytes 1769480 | tf_op jit(solution)/shard_map/ppermute | solution.py:46
  96.8 28.6 %collective-permute-start.3 = (bf16[8,24,1664]{2,1,0:T(8,128)(2,1)S(1)}, bf16[8,24,1664]{2,1,0:T(8,128)(2,1)S(1)}, u32[]{:S(2)}, u32[]{:S(2)}) collective-permute-start(bf16[8,24,1664]{2,1,0:T(8,128)(2,1)S(1)} %bitcast.844), channel_id=1, source_target_pairs={{0,2},{1,3},{2,0},{3,1},{4,6},{5,7},{6,4},{7,5},{8,10},{9,11},{10,... | collective-permute-start | bytes 1916936 | tf_op jit(solution)/shard_map/ppermute | solution.py:46
  98.9 36.1 %collective-permute-start.23 = (bf16[8,24,2048]{2,1,0:T(8,128)(2,1)S(1)}, bf16[8,24,2048]{2,1,0:T(8,128)(2,1)S(1)}, u32[]{:S(2)}, u32[]{:S(2)}) collective-permute-start(bf16[8,24,2048]{2,1,0:T(8,128)(2,1)S(1)} %bitcast.837), channel_id=1, source_target_pairs={{0,2},{1,3},{2,0},{3,1},{4,6},{5,7},{6,4},{7,5},{8,10},{9,11},{10,... | collective-permute-start | bytes 2359304 | tf_op jit(solution)/shard_map/ppermute | solution.py:46
  111.5 24.5 %collective-permute-start.28 = (bf16[8,24,2048]{2,1,0:T(8,128)(2,1)S(1)}, bf16[8,24,2048]{2,1,0:T(8,128)(2,1)S(1)}, u32[]{:S(2)}, u32[]{:S(2)}) collective-permute-start(bf16[8,24,2048]{2,1,0:T(8,128)(2,1)S(1)} %bitcast.900), channel_id=1, source_target_pairs={{0,4},{1,5},{2,6},{3,7},{4,0},{5,1},{6,2},{7,3},{8,12},{9,13},{10,... | collective-permute-start | bytes 2359304 | tf_op jit(solution)/shard_map/ppermute | solution.py:46
  124.2 15.0 %collective-permute-start.34 = (bf16[16,64,384]{2,1,0:T(8,128)(2,1)S(1)}, bf16[16,64,384]{2,1,0:T(8,128)(2,1)S(1)}, u32[]{:S(2)}, u32[]{:S(2)}) collective-permute-start(bf16[16,64,384]{2,1,0:T(8,128)(2,1)S(1)} %bitcast.835), channel_id=1, source_target_pairs={{0,1},{1,0},{2,3},{3,2},{4,5},{5,4},{6,7},{7,6},{8,9},{9,8},{10,11... | collective-permute-start | bytes 2359304 | tf_op jit(solution)/shard_map/ppermute | solution.py:46
  124.5 17.1 %collective-permute-start.39 = (bf16[16,64,384]{2,1,0:T(8,128)(2,1)S(1)}, bf16[16,64,384]{2,1,0:T(8,128)(2,1)S(1)}, u32[]{:S(2)}, u32[]{:S(2)}) collective-permute-start(bf16[16,64,384]{2,1,0:T(8,128)(2,1)S(1)} %bitcast.836), channel_id=1, source_target_pairs={{0,1},{1,0},{2,3},{3,2},{4,5},{5,4},{6,7},{7,6},{8,9},{9,8},{10,11... | collective-permute-start | bytes 2359304 | tf_op jit(solution)/shard_map/ppermute | solution.py:46
  125.4 18.6 %collective-permute-start.14 = (bf16[16,24,1536]{2,1,0:T(8,128)(2,1)S(1)}, bf16[16,24,1536]{2,1,0:T(8,128)(2,1)S(1)}, u32[]{:S(2)}, u32[]{:S(2)}) collective-permute-start(bf16[16,24,1536]{2,1,0:T(8,128)(2,1)S(1)} %bitcast.803), channel_id=1, source_target_pairs={{0,1},{1,0},{2,3},{3,2},{4,5},{5,4},{6,7},{7,6},{8,9},{9,8},{10,11... | collective-permute-start | bytes 3538952 | tf_op jit(solution)/shard_map/ppermute | solution.py:46
  135.0 11.7 %collective-permute-start.9 = (bf16[16,24,1536]{2,1,0:T(8,128)(2,1)S(1)}, bf16[16,24,1536]{2,1,0:T(8,128)(2,1)S(1)}, u32[]{:S(2)}, u32[]{:S(2)}) collective-permute-start(bf16[16,24,1536]{2,1,0:T(8,128)(2,1)S(1)} %bitcast.804), channel_id=1, source_target_pairs={{0,1},{1,0},{2,3},{3,2},{4,5},{5,4},{6,7},{7,6},{8,9},{9,8},{10,11... | collective-permute-start | bytes 3538952 | tf_op jit(solution)/shard_map/ppermute | solution.py:46
  136.0 12.8 %collective-permute-start.19 = (bf16[16,24,1536]{2,1,0:T(8,128)(2,1)S(1)}, bf16[16,24,1536]{2,1,0:T(8,128)(2,1)S(1)}, u32[]{:S(2)}, u32[]{:S(2)}) collective-permute-start(bf16[16,24,1536]{2,1,0:T(8,128)(2,1)S(1)} %bitcast.805), channel_id=1, source_target_pairs={{0,1},{1,0},{2,3},{3,2},{4,5},{5,4},{6,7},{7,6},{8,9},{9,8},{10,11... | collective-permute-start | bytes 3538952 | tf_op jit(solution)/shard_map/ppermute | solution.py:46
  139.1 12.6 %collective-permute-start.4 = (bf16[16,24,1664]{2,1,0:T(8,128)(2,1)}, bf16[16,24,1664]{2,1,0:T(8,128)(2,1)}, u32[]{:S(2)}, u32[]{:S(2)}) collective-permute-start(bf16[16,24,1664]{2,1,0:T(8,128)(2,1)} %bitcast.20), channel_id=1, source_target_pairs={{0,1},{1,0},{2,3},{3,2},{4,5},{5,4},{6,7},{7,6},{8,9},{9,8},{10,11... | collective-permute-start | bytes 3833864 | tf_op jit(solution)/shard_map/ppermute | solution.py:46
  141.6 33.1 %collective-permute-start.24 = (bf16[16,24,2048]{2,1,0:T(8,128)(2,1)}, bf16[16,24,2048]{2,1,0:T(8,128)(2,1)}, u32[]{:S(2)}, u32[]{:S(2)}) collective-permute-start(bf16[16,24,2048]{2,1,0:T(8,128)(2,1)} %bitcast.112), channel_id=1, source_target_pairs={{0,1},{1,0},{2,3},{3,2},{4,5},{5,4},{6,7},{7,6},{8,9},{9,8},{10,11... | collective-permute-start | bytes 4718600 | tf_op jit(solution)/shard_map/ppermute | solution.py:46
  144.0 33.6 %collective-permute-start.29 = (bf16[16,24,2048]{2,1,0:T(8,128)(2,1)}, bf16[16,24,2048]{2,1,0:T(8,128)(2,1)}, u32[]{:S(2)}, u32[]{:S(2)}) collective-permute-start(bf16[16,24,2048]{2,1,0:T(8,128)(2,1)} %bitcast.129), channel_id=1, source_target_pairs={{0,1},{1,0},{2,3},{3,2},{4,5},{5,4},{6,7},{7,6},{8,9},{9,8},{10,11... | collective-permute-start | bytes 4718600 | tf_op jit(solution)/shard_map/ppermute | solution.py:46
  246.2 14.0 %collective-permute-start.100 = (f32[35,768]{1,0:T(8,128)S(1)}, f32[35,768]{1,0:T(8,128)S(1)}, u32[]{:S(2)}, u32[]{:S(2)}) collective-permute-start(f32[35,768]{1,0:T(8,128)S(1)} %select_maximum_fusion), channel_id=1, source_target_pairs={{0,1},{1,0},{2,3},{3,2},{4,5},{5,4},{6,7},{7,6},{8,9},{9,8},{10,11... | collective-permute-start | bytes 322568 | tf_op jit(solution)/shard_map/ppermute | solution.py:77
  247.5 52.0 %collective-permute-start.90 = (bf16[16,1,64,384]{3,2,0,1:T(8,128)(2,1)}, bf16[16,1,64,384]{3,2,0,1:T(8,128)(2,1)}, u32[]{:S(2)}, u32[]{:S(2)}) collective-permute-start(bf16[16,1,64,384]{3,2,0,1:T(8,128)(2,1)} %dynamic-slice_bitcast_fusion.3), channel_id=1, source_target_pairs={{0,1},{1,0},{2,3},{3,2},{4,5},{5,4},{6,7},{7,6},{8,9},{9,8},{10,11... | collective-permute-start | bytes 2359304 | tf_op jit(solution)/shard_map/ppermute | solution.py:68
  248.8 53.9 %collective-permute-start.95 = (bf16[16,1,64,384]{3,2,0,1:T(8,128)(2,1)}, bf16[16,1,64,384]{3,2,0,1:T(8,128)(2,1)}, u32[]{:S(2)}, u32[]{:S(2)}) collective-permute-start(bf16[16,1,64,384]{3,2,0,1:T(8,128)(2,1)} %dynamic-slice_bitcast_fusion.2), channel_id=1, source_target_pairs={{0,1},{1,0},{2,3},{3,2},{4,5},{5,4},{6,7},{7,6},{8,9},{9,8},{10,11... | collective-permute-start | bytes 2359304 | tf_op jit(solution)/shard_map/ppermute | solution.py:68
  253.6 32.5 %collective-permute-start.75 = (bf16[16,1,24,768]{3,2,0,1:T(8,128)(2,1)}, bf16[16,1,24,768]{3,2,0,1:T(8,128)(2,1)}, u32[]{:S(2)}, u32[]{:S(2)}) collective-permute-start(bf16[16,1,24,768]{3,2,0,1:T(8,128)(2,1)} %dynamic-slice_bitcast_fusion.6), channel_id=1, source_target_pairs={{0,1},{1,0},{2,3},{3,2},{4,5},{5,4},{6,7},{7,6},{8,9},{9,8},{10,11... | collective-permute-start | bytes 1769480 | tf_op jit(solution)/shard_map/ppermute | solution.py:68
  254.9 33.2 %collective-permute-start.70 = (bf16[16,1,24,768]{3,2,0,1:T(8,128)(2,1)}, bf16[16,1,24,768]{3,2,0,1:T(8,128)(2,1)}, u32[]{:S(2)}, u32[]{:S(2)}) collective-permute-start(bf16[16,1,24,768]{3,2,0,1:T(8,128)(2,1)} %dynamic-slice_bitcast_fusion.7), channel_id=1, source_target_pairs={{0,1},{1,0},{2,3},{3,2},{4,5},{5,4},{6,7},{7,6},{8,9},{9,8},{10,11... | collective-permute-start | bytes 1769480 | tf_op jit(solution)/shard_map/ppermute | solution.py:68
  275.8 9.0 %collective-permute-start.104 = (f32[35,768]{1,0:T(8,128)S(1)}, f32[35,768]{1,0:T(8,128)S(1)}, u32[]{:S(2)}, u32[]{:S(2)}) collective-permute-start(f32[35,768]{1,0:T(8,128)S(1)} %add.557), channel_id=1, source_target_pairs={{0,16},{1,17},{2,18},{3,19},{4,20},{5,21},{6,22},{7,23},{8,24},{9,... | collective-permute-start | bytes 322568 | tf_op jit(solution)/shard_map/ppermute | solution.py:77
  291.8 184.3 %collective-permute-start.85 = (bf16[16,1,24,2048]{3,2,0,1:T(8,128)(2,1)S(1)}, bf16[16,1,24,2048]{3,2,0,1:T(8,128)(2,1)S(1)}, u32[]{:S(2)}, u32[]{:S(2)}) collective-permute-start(bf16[16,1,24,2048]{3,2,0,1:T(8,128)(2,1)S(1)} %copy-done.73), channel_id=1, source_target_pairs={{0,1},{1,0},{2,3},{3,2},{4,5},{5,4},{6,7},{7,6},{8,9},{9,8},{10,11... | collective-permute-start | bytes 4718600 | tf_op jit(solution)/shard_map/ppermute | solution.py:68
  293.2 183.8 %collective-permute-start.80 = (bf16[16,1,24,2048]{3,2,0,1:T(8,128)(2,1)S(1)}, bf16[16,1,24,2048]{3,2,0,1:T(8,128)(2,1)S(1)}, u32[]{:S(2)}, u32[]{:S(2)}) collective-permute-start(bf16[16,1,24,2048]{3,2,0,1:T(8,128)(2,1)S(1)} %copy-done.72), channel_id=1, source_target_pairs={{0,1},{1,0},{2,3},{3,2},{4,5},{5,4},{6,7},{7,6},{8,9},{9,8},{10,11... | collective-permute-start | bytes 4718600 | tf_op jit(solution)/shard_map/ppermute | solution.py:68
  299.0 9.9 %collective-permute-start.76 = (bf16[8,1,24,768]{3,2,0,1:T(8,128)(2,1)S(1)}, bf16[8,1,24,768]{3,2,0,1:T(8,128)(2,1)S(1)}, u32[]{:S(2)}, u32[]{:S(2)}) collective-permute-start(bf16[8,1,24,768]{3,2,0,1:T(8,128)(2,1)S(1)} %dynamic-slice_bitcast_fusion.17), channel_id=1, source_target_pairs={{0,2},{1,3},{2,0},{3,1},{4,6},{5,7},{6,4},{7,5},{8,10},{9,11},{10,... | collective-permute-start | bytes 884744 | tf_op jit(solution)/shard_map/ppermute | solution.py:68
  299.6 10.9 %collective-permute-start.71 = (bf16[4,2,24,768]{3,2,1,0:T(8,128)(2,1)S(1)}, bf16[4,2,24,768]{3,2,1,0:T(8,128)(2,1)S(1)}, u32[]{:S(2)}, u32[]{:S(2)}) collective-permute-start(bf16[4,2,24,768]{3,2,1,0:T(8,128)(2,1)S(1)} %dynamic-slice_bitcast_fusion.18), channel_id=1, source_target_pairs={{0,4},{1,5},{2,6},{3,7},{4,0},{5,1},{6,2},{7,3},{8,12},{9,13},{10,... | collective-permute-start | bytes 884744 | tf_op jit(solution)/shard_map/ppermute | solution.py:68
  302.7 12.5 %collective-permute-start.66 = (bf16[8,1,24,768]{3,2,0,1:T(8,128)(2,1)S(1)}, bf16[8,1,24,768]{3,2,0,1:T(8,128)(2,1)S(1)}, u32[]{:S(2)}, u32[]{:S(2)}) collective-permute-start(bf16[8,1,24,768]{3,2,0,1:T(8,128)(2,1)S(1)} %dynamic-slice_bitcast_fusion.19), channel_id=1, source_target_pairs={{0,2},{1,3},{2,0},{3,1},{4,6},{5,7},{6,4},{7,5},{8,10},{9,11},{10,... | collective-permute-start | bytes 884744 | tf_op jit(solution)/shard_map/ppermute | solution.py:68
  308.9 8.0 %collective-permute-start.61 = (bf16[4,2,24,768]{3,2,1,0:T(8,128)(2,1)S(1)}, bf16[4,2,24,768]{3,2,1,0:T(8,128)(2,1)S(1)}, u32[]{:S(2)}, u32[]{:S(2)}) collective-permute-start(bf16[4,2,24,768]{3,2,1,0:T(8,128)(2,1)S(1)} %dynamic-slice_bitcast_fusion.20), channel_id=1, source_target_pairs={{0,4},{1,5},{2,6},{3,7},{4,0},{5,1},{6,2},{7,3},{8,12},{9,13},{10,... | collective-permute-start | bytes 884744 | tf_op jit(solution)/shard_map/ppermute | solution.py:68
  310.5 10.2 %collective-permute-start.56 = (bf16[8,1,24,768]{3,2,0,1:T(8,128)(2,1)S(1)}, bf16[8,1,24,768]{3,2,0,1:T(8,128)(2,1)S(1)}, u32[]{:S(2)}, u32[]{:S(2)}) collective-permute-start(bf16[8,1,24,768]{3,2,0,1:T(8,128)(2,1)S(1)} %dynamic-slice_bitcast_fusion.21), channel_id=1, source_target_pairs={{0,2},{1,3},{2,0},{3,1},{4,6},{5,7},{6,4},{7,5},{8,10},{9,11},{10,... | collective-permute-start | bytes 884744 | tf_op jit(solution)/shard_map/ppermute | solution.py:68
  315.2 9.9 %collective-permute-start.51 = (bf16[4,2,24,768]{3,2,1,0:T(8,128)(2,1)S(1)}, bf16[4,2,24,768]{3,2,1,0:T(8,128)(2,1)S(1)}, u32[]{:S(2)}, u32[]{:S(2)}) collective-permute-start(bf16[4,2,24,768]{3,2,1,0:T(8,128)(2,1)S(1)} %dynamic-slice_bitcast_fusion.22), channel_id=1, source_target_pairs={{0,4},{1,5},{2,6},{3,7},{4,0},{5,1},{6,2},{7,3},{8,12},{9,13},{10,... | collective-permute-start | bytes 884744 | tf_op jit(solution)/shard_map/ppermute | solution.py:68
  316.8 12.0 %collective-permute-start.46 = (bf16[4,2,24,768]{3,2,1,0:T(8,128)(2,1)S(1)}, bf16[4,2,24,768]{3,2,1,0:T(8,128)(2,1)S(1)}, u32[]{:S(2)}, u32[]{:S(2)}) collective-permute-start(bf16[4,2,24,768]{3,2,1,0:T(8,128)(2,1)S(1)} %dynamic-slice_bitcast_fusion.23), channel_id=1, source_target_pairs={{0,4},{1,5},{2,6},{3,7},{4,0},{5,1},{6,2},{7,3},{8,12},{9,13},{10,... | collective-permute-start | bytes 884744 | tf_op jit(solution)/shard_map/ppermute | solution.py:68
  320.7 9.9 %collective-permute-start.41 = (bf16[8,1,24,768]{3,2,0,1:T(8,128)(2,1)S(1)}, bf16[8,1,24,768]{3,2,0,1:T(8,128)(2,1)S(1)}, u32[]{:S(2)}, u32[]{:S(2)}) collective-permute-start(bf16[8,1,24,768]{3,2,0,1:T(8,128)(2,1)S(1)} %dynamic-slice_bitcast_fusion.24), channel_id=1, source_target_pairs={{0,2},{1,3},{2,0},{3,1},{4,6},{5,7},{6,4},{7,5},{8,10},{9,11},{10,... | collective-permute-start | bytes 884744 | tf_op jit(solution)/shard_map/ppermute | solution.py:68
  325.1 127.8 %collective-permute-start.91 = (bf16[8,1,64,384]{3,2,0,1:T(8,128)(2,1)S(1)}, bf16[8,1,64,384]{3,2,0,1:T(8,128)(2,1)S(1)}, u32[]{:S(2)}, u32[]{:S(2)}) collective-permute-start(bf16[8,1,64,384]{3,2,0,1:T(8,128)(2,1)S(1)} %dynamic-slice_bitcast_fusion.15), channel_id=1, source_target_pairs={{0,2},{1,3},{2,0},{3,1},{4,6},{5,7},{6,4},{7,5},{8,10},{9,11},{10,... | collective-permute-start | bytes 1179656 | tf_op jit(solution)/shard_map/ppermute | solution.py:68
  328.9 125.7 %collective-permute-start.96 = (bf16[4,2,64,384]{3,2,1,0:T(8,128)(2,1)S(1)}, bf16[4,2,64,384]{3,2,1,0:T(8,128)(2,1)S(1)}, u32[]{:S(2)}, u32[]{:S(2)}) collective-permute-start(bf16[4,2,64,384]{3,2,1,0:T(8,128)(2,1)S(1)} %dynamic-slice_bitcast_fusion.14), channel_id=1, source_target_pairs={{0,4},{1,5},{2,6},{3,7},{4,0},{5,1},{6,2},{7,3},{8,12},{9,13},{10,... | collective-permute-start | bytes 1179656 | tf_op jit(solution)/shard_map/ppermute | solution.py:68
  330.6 10.1 %collective-permute-start.77 = (bf16[4,1,24,768]{3,2,0,1:T(8,128)(2,1)S(1)}, bf16[4,1,24,768]{3,2,0,1:T(8,128)(2,1)S(1)}, u32[]{:S(2)}, u32[]{:S(2)}) collective-permute-start(bf16[4,1,24,768]{3,2,0,1:T(8,128)(2,1)S(1)} %dynamic-slice_bitcast_fusion.28), channel_id=1, source_target_pairs={{0,4},{1,5},{2,6},{3,7},{4,0},{5,1},{6,2},{7,3},{8,12},{9,13},{10,... | collective-permute-start | bytes 442376 | tf_op jit(solution)/shard_map/ppermute | solution.py:68
  453.0 7.8 %collective-permute-start.92 = (bf16[4,1,64,384]{3,2,0,1:T(8,128)(2,1)S(1)}, bf16[4,1,64,384]{3,2,0,1:T(8,128)(2,1)S(1)}, u32[]{:S(2)}, u32[]{:S(2)}) collective-permute-start(bf16[4,1,64,384]{3,2,0,1:T(8,128)(2,1)S(1)} %dynamic-slice_bitcast_fusion.25), channel_id=1, source_target_pairs={{0,4},{1,5},{2,6},{3,7},{4,0},{5,1},{6,2},{7,3},{8,12},{9,13},{10,... | collective-permute-start | bytes 589832 | tf_op jit(solution)/shard_map/ppermute | solution.py:68
  454.8 7.6 %collective-permute-start.97 = (bf16[4,1,64,384]{3,2,1,0:T(8,128)(2,1)S(1)}, bf16[4,1,64,384]{3,2,1,0:T(8,128)(2,1)S(1)}, u32[]{:S(2)}, u32[]{:S(2)}) collective-permute-start(bf16[4,1,64,384]{3,2,1,0:T(8,128)(2,1)S(1)} %constant_dynamic-slice_fusion.2), channel_id=1, source_target_pairs={{0,2},{1,3},{2,0},{3,1},{4,6},{5,7},{6,4},{7,5},{8,10},{9,11},{10,... | collective-permute-start | bytes 589832 | tf_op jit(solution)/shard_map/ppermute | solution.py:68
  476.9 12.1 %collective-permute-start.86 = (bf16[4,2,24,2048]{3,2,1,0:T(8,128)(2,1)S(1)}, bf16[4,2,24,2048]{3,2,1,0:T(8,128)(2,1)S(1)}, u32[]{:S(2)}, u32[]{:S(2)}) collective-permute-start(bf16[4,2,24,2048]{3,2,1,0:T(8,128)(2,1)S(1)} %dynamic-slice_bitcast_fusion.4), channel_id=1, source_target_pairs={{0,4},{1,5},{2,6},{3,7},{4,0},{5,1},{6,2},{7,3},{8,12},{9,13},{10,... | collective-permute-start | bytes 2359304 | tf_op jit(solution)/shard_map/ppermute | solution.py:68
  477.7 12.1 %collective-permute-start.81 = (bf16[8,1,24,2048]{3,2,0,1:T(8,128)(2,1)S(1)}, bf16[8,1,24,2048]{3,2,0,1:T(8,128)(2,1)S(1)}, u32[]{:S(2)}, u32[]{:S(2)}) collective-permute-start(bf16[8,1,24,2048]{3,2,0,1:T(8,128)(2,1)S(1)} %dynamic-slice_bitcast_fusion.5), channel_id=1, source_target_pairs={{0,2},{1,3},{2,0},{3,1},{4,6},{5,7},{6,4},{7,5},{8,10},{9,11},{10,... | collective-permute-start | bytes 2359304 | tf_op jit(solution)/shard_map/ppermute | solution.py:68
  489.3 7.8 %collective-permute-start.87 = (bf16[4,1,24,2048]{3,2,1,0:T(8,128)(2,1)S(1)}, bf16[4,1,24,2048]{3,2,1,0:T(8,128)(2,1)S(1)}, u32[]{:S(2)}, u32[]{:S(2)}) collective-permute-start(bf16[4,1,24,2048]{3,2,1,0:T(8,128)(2,1)S(1)} %constant_dynamic-slice_fusion.5), channel_id=1, source_target_pairs={{0,2},{1,3},{2,0},{3,1},{4,6},{5,7},{6,4},{7,5},{8,10},{9,11},{10,... | collective-permute-start | bytes 1179656 | tf_op jit(solution)/shard_map/ppermute | solution.py:68
  490.1 8.5 %collective-permute-start.82 = (bf16[4,1,24,2048]{3,2,0,1:T(8,128)(2,1)S(1)}, bf16[4,1,24,2048]{3,2,0,1:T(8,128)(2,1)S(1)}, u32[]{:S(2)}, u32[]{:S(2)}) collective-permute-start(bf16[4,1,24,2048]{3,2,0,1:T(8,128)(2,1)S(1)} %dynamic-slice_bitcast_fusion.16), channel_id=1, source_target_pairs={{0,4},{1,5},{2,6},{3,7},{4,0},{5,1},{6,2},{7,3},{8,12},{9,13},{10,... | collective-permute-start | bytes 1179656 | tf_op jit(solution)/shard_map/ppermute | solution.py:68
  (139 other events, 723.6 us)

commit v2 on v1

v2 whole, which is shorter than its diff:
```python
from functools import partial

import jax
import jax.numpy as jnp
from jax import lax
from jax.experimental import pallas as pl
from jax.experimental.pallas import tpu as pltpu
from jax.sharding import PartitionSpec as P

H = 12
AXIS = "dp"
EPSILON = 1e-06
MASKED = -1e30
BF = jnp.bfloat16
F32 = jnp.float32


def matmul(left, right):
    return jnp.dot(left, right, preferred_element_type=F32)


def matmul_nt(left, right):
    return lax.dot_general(left, right, (((1,), (1,)), ((), ())), preferred_element_type=F32)


def matmul_tn(left, right):
    return lax.dot_general(left, right, (((0,), (0,)), ((), ())), preferred_element_type=F32)


def partner(count, bit):
    return [(i, i ^ (1 << bit)) for i in range(count)]


def own_bit(bit):
    return (lax.axis_index(AXIS) >> bit) & 1


def tied(*values):
    return lax.optimization_barrier(values)


def split_bits(count):
    bits = count.bit_length() - 1
    assert 1 << bits == count and bits > 2
    return list(range(bits - 1, 2, -1)), (2, 1), 0


def swap_blocks(held, done, bit, count):
    other = lax.ppermute(held, AXIS, partner(count, bit))
    rows, columns = held.shape[1:]
    low = 1 << sum(1 for b in done if b < bit)
    shape = (held.shape[0] // low, 1, low, rows, columns)
    mine, theirs = held.reshape(shape), other.reshape(shape)
    upper = own_bit(bit) == 1
    return jnp.concatenate(
        [jnp.where(upper, theirs, mine), jnp.where(upper, mine, theirs)], axis=1
    ).reshape(-1, rows, columns)


def gather_high(piece, count):
    high, _, _ = split_bits(count)
    held, done = piece[None], []
    for bit in high:
        held = swap_blocks(held, done, bit, count)
        done.append(bit)
    return held


def gather_middle(held, cut, count):
    high, (left, right), _ = split_bits(count)
    halves = []
    for part, pair in ((held[:, :, :cut], (left, right)), (held[:, :, cut:], (right, left))):
        done = list(high)
        for bit in pair:
            part = swap_blocks(part, done, bit, count)
            done.append(bit)
        halves.append(part)
    return halves


def gather_last(halves, count):
    high, middle, lowest = split_bits(count)
    done = [*high, *middle]
    return [swap_blocks(p, done, lowest, count).reshape(-1, p.shape[2]) for p in halves]


def fold(held, left, bit, count, last=False):
    rows, columns = held.shape[1:]
    low = 1 << sum(1 for b in left if b < bit)
    view = held.reshape(held.shape[0] // (2 * low), 2, low, rows, columns)
    mine = own_bit(bit)
    sent = lax.dynamic_index_in_dim(view, 1 - mine, 1, keepdims=False)
    kept = lax.dynamic_index_in_dim(view, mine, 1, keepdims=False)
    got = lax.ppermute(sent, AXIS, partner(count, bit))
    total = kept.astype(F32) + got.astype(F32)
    return (total if last else total.astype(BF)).reshape(-1, rows, columns)


class Reduction:
    def __init__(self, first, second, count):
        rows = first.shape[0] // count
        self.count, self.step = count, 0
        self.parts = [t.reshape(count, rows, t.shape[1]) for t in (first, second)]
        high, (one, two), lowest = split_bits(count)
        self.high = high[::-1]
        self.orders = ((lowest, one, two), (lowest, two, one))
        self.left = [list(range(count.bit_length() - 1)) for _ in range(2)]

    def advance(self):
        if self.step < 3:
            for side in range(2):
                bit = self.orders[side][self.step]
                self.parts[side] = fold(self.parts[side], self.left[side], bit, self.count)
                self.left[side].remove(bit)
        else:
            if self.step == 3:
                self.parts = [jnp.concatenate(self.parts, axis=2)]
            bit = self.high[self.step - 3]
            last = self.step - 2 == len(self.high)
            self.parts = [fold(self.parts[0], self.left[0], bit, self.count, last)]
            self.left[0].remove(bit)
        self.step += 1

    def tie(self, *values):
        out = tied(*self.parts, *values)
        self.parts = list(out[: len(self.parts)])
        return out[len(self.parts) :]

    def finish(self):
        while self.left[0]:
            self.advance()
        return self.parts[0][0]


def total_sum(values, count):
    for bit in range(count.bit_length() - 1):
        values = values + lax.ppermute(values, AXIS, partner(count, bit))
    return values


def norm_scale_of(hidden):
    return lax.rsqrt(jnp.mean(hidden * hidden, axis=-1, keepdims=True) + EPSILON)


def norm_backward(hidden, gain, cotangent):
    scale = norm_scale_of(hidden)
    weighted = gain * cotangent
    grad_gain = jnp.sum(cotangent * hidden * scale, axis=0, keepdims=True)
    inner = jnp.mean(weighted * hidden, axis=-1, keepdims=True)
    return scale * weighted - hidden * (scale * scale * scale) * inner, grad_gain


def toeplitz(vector):
    length = vector.shape[0]
    padded = jnp.concatenate([vector[::-1], jnp.zeros((length,), vector.dtype)])
    flattened = jnp.tile(padded, length + 1)[length - 1 : length - 1 + length * (2 * length - 1)]
    return flattened.reshape(length, 2 * length - 1)[:, :length]


def segment_ids(lengths, row_total):
    boundary = jnp.cumsum(lengths)
    row_index = jnp.arange(row_total, dtype=jnp.int32)
    return jnp.sum((row_index[:, None] >= boundary[None, :]).astype(jnp.int32), axis=1)


LANES = 128


def pair_stack(block, per_head):
    first = lax.broadcasted_iota(jnp.int32, block.shape, 1) < per_head
    zero = jnp.zeros_like(block)
    return jnp.concatenate([jnp.where(first, block, zero), jnp.where(first, zero, block)], axis=0)


def side_by_side(stacked):
    rows = stacked.shape[0] // 2
    return jnp.concatenate([stacked[:rows], stacked[rows:]], axis=1)


def attention_pair(query, key, value, bias, per_head):
    scores = matmul_nt(pair_stack(query, per_head), key) + bias
    highest = jnp.max(scores, axis=1, keepdims=True)
    total = jnp.sum(jnp.exp(scores - highest), axis=1, keepdims=True)
    weights = jnp.exp(scores - (highest + jnp.log(total)))
    mixed = matmul(side_by_side(weights.astype(BF)), pair_stack(value, per_head)).astype(BF)
    return mixed, weights


def attention_pair_grad(query, key, value, mixed, grad, weights, per_head):
    product = grad.astype(F32) * mixed.astype(F32)
    first = lax.broadcasted_iota(jnp.int32, product.shape, 1) < per_head
    row_dot = jnp.concatenate(
        [
            jnp.sum(jnp.where(first, product, 0.0), axis=1, keepdims=True),
            jnp.sum(jnp.where(first, 0.0, product), axis=1, keepdims=True),
        ],
        axis=0,
    )
    grad_stack = pair_stack(grad, per_head)
    grad_scores = weights * (matmul_nt(grad_stack, value) - row_dot)
    low = grad_scores.astype(BF)
    grad_query = matmul(side_by_side(low), pair_stack(key, per_head)).astype(BF)
    grad_key = matmul_tn(low, pair_stack(query, per_head)).astype(BF)
    grad_value = matmul_tn(weights.astype(BF), grad_stack).astype(BF)
    return grad_query, grad_key, grad_value, grad_scores


SUBLANES = 8


def tile_block(width, inner):
    block = SUBLANES
    while block * inner % (width * SUBLANES):
        block += SUBLANES
    return block


def to_tiles(array, block, inner):
    width = array.shape[1]
    deep = block * inner // width
    tiles = array.reshape(-1, deep // SUBLANES, SUBLANES, width // LANES, LANES)
    tiles = tiles.transpose(0, 1, 3, 2, 4)
    tiles = tiles.reshape(-1, block // SUBLANES, inner // LANES, SUBLANES, LANES)
    return tiles.transpose(0, 1, 3, 2, 4).reshape(-1, inner)


def from_tiles(array, block, width):
    inner = array.shape[1]
    deep = block * inner // width
    tiles = array.reshape(-1, block // SUBLANES, SUBLANES, inner // LANES, LANES)
    tiles = tiles.transpose(0, 1, 3, 2, 4)
    tiles = tiles.reshape(-1, deep // SUBLANES, width // LANES, SUBLANES, LANES)
    return tiles.transpose(0, 1, 3, 2, 4).reshape(-1, width)


def tile_runs(block, width, inner):
    runs, wide, deep = [], width // LANES, inner // LANES
    for tile in range(block // SUBLANES * deep):
        here = (tile // deep, tile // wide)
        if runs and runs[-1][0] == here:
            runs[-1][3] += LANES
        else:
            runs.append([here, tile % deep * LANES, tile % wide * LANES, LANES])
    return [(h[0] * SUBLANES, c, h[1] * SUBLANES, d, n) for h, c, d, n in runs]


def diagonal_sums(block):
    rows, columns = block.shape
    while rows > 1:
        rows //= 2
        block = block[:rows] + pltpu.roll(block[rows:], (columns - rows) % columns, 1)
    return block


def gain_rows_of(columns):
    return columns.astype(F32).T


def self_forward(per_head, x_ref, wa_ref, wb_ref, bias_ref,
                 gains_ref, normed_ref, qkv_ref, mixed_ref, weights_ref, resid_ref):
    width = x_ref.shape[1]
    rows = x_ref.shape[0]
    gains = gain_rows_of(wa_ref[:, 2 * width :])[:8]
    gains_ref[...] = gains
    resid = x_ref[...].astype(F32)
    normed = (resid * norm_scale_of(resid) * gains[0:1]).astype(BF)
    normed_ref[...] = normed
    qkv_ref[:, : 2 * width] = matmul(normed, wa_ref[:, : 2 * width]).astype(BF)
    qkv_ref[:, 2 * width :] = matmul(normed, wb_ref[:, :width]).astype(BF)
    for pair in range(width // (2 * per_head)):
        at = pl.ds(pair * 2 * per_head, 2 * per_head)
        key_at = pl.ds(width + pair * 2 * per_head, 2 * per_head)
        value_at = pl.ds(2 * width + pair * 2 * per_head, 2 * per_head)
        mixed, weights = attention_pair(
            qkv_ref[:, at], qkv_ref[:, key_at], qkv_ref[:, value_at],
            bias_ref[pl.ds(pair * 2 * rows, 2 * rows), :], per_head,
        )
        mixed_ref[:, at] = mixed
        weights_ref[pl.ds(pair * 2 * rows, 2 * rows), :] = weights
    resid_ref[...] = resid + matmul(mixed_ref[...], wb_ref[:, width:])


def cross_forward(per_head, resid_ref, enc_ref, wa_ref, wb_ref, gains_ref, mask_ref,
                  normed_ref, rows_ref, kv_ref, mixed_ref, weights_ref, out_ref, next_ref):
    rows, width = resid_ref.shape
    resid = resid_ref[...]
    normed = (resid * norm_scale_of(resid) * gains_ref[1:2, :]).astype(BF)
    normed_ref[...] = normed
    rows_ref[...] = matmul(normed, wb_ref[:, :width]).astype(BF)
    kv_ref[...] = matmul(enc_ref[...], wa_ref[...]).astype(BF)
    mask = jnp.concatenate([mask_ref[...], mask_ref[...]], axis=0)
    for pair in range(width // (2 * per_head)):
        at = pl.ds(pair * 2 * per_head, 2 * per_head)
        value_at = pl.ds(width + pair * 2 * per_head, 2 * per_head)
        mixed, weights = attention_pair(
            rows_ref[:, at], kv_ref[:, at], kv_ref[:, value_at], mask, per_head
        )
        mixed_ref[:, at] = mixed
        weights_ref[pl.ds(pair * 2 * rows, 2 * rows), :] = weights
    resid = resid + matmul(mixed_ref[...], wb_ref[:, width:])
    out_ref[...] = resid
    next_ref[...] = (resid * norm_scale_of(resid) * gains_ref[2:3, :]).astype(BF)


def feed_step(chunk, block, resid_ref, normed_ref, grad_ref, gains_ref, feed_ref,
              out_ref, grad_resid_ref, grad_gain_ref, terms_ref,
              weights, down, terms, terms_down, in_sem, down_sem, out_sem, down_out_sem):
    width = resid_ref.shape[1]
    inner = down.shape[0]
    steps = inner // chunk
    deep = block * inner // width
    runs = tile_runs(block, width, inner)

    def columns(step, side):
        return pl.ds(side * inner + step * chunk, chunk)

    def load(step, side):
        at = columns(step, side)
        return pltpu.make_async_copy(feed_ref.at[:, at], weights.at[:, at], in_sem.at[step, side])

    def save(step, side):
        at = columns(step, side)
        return pltpu.make_async_copy(terms.at[:, at], terms_ref.at[:, at], out_sem.at[step, side])

    def tile_copies(group, sides, hbm, vmem, sem):
        for row, column, to_row, to_column, length in runs:
            far = hbm.at[
                pl.ds(pl.multiple_of(group * block + row, SUBLANES), SUBLANES),
                pl.ds(2 * inner + column, length),
            ]
            near = vmem.at[
                pl.ds(pl.multiple_of(group * deep + to_row, SUBLANES), SUBLANES),
                pl.ds(to_column, length),
            ]
            pltpu.make_async_copy(*((far, near) if sides == 0 else (near, far)), sem).start()

    for side in range(2):
        load(0, side).start()

    def fetch_down(group, carry):
        tile_copies(group, 0, feed_ref, down, down_sem)
        return carry

    lax.fori_loop(0, inner // deep, fetch_down, 0)
    for step in range(1, steps):
        for side in range(2):
            load(step, side).start()
    normed, grad = normed_ref[...], grad_ref[...]
    total = resid_ref[...]
    grad_normed = jnp.zeros_like(total)
    for step in range(steps):
        at, next_at = slice(step * chunk, (step + 1) * chunk), slice(
            inner + step * chunk, inner + (step + 1) * chunk
        )
        for side in range(2):
            load(step, side).wait()
        gate = matmul(normed, weights[:, at])
        linear = matmul(normed, weights[:, next_at])
        square = gate * gate
        bend = jnp.tanh(0.7978845608 * gate * (1.0 + 0.044715 * square))
        half = 0.5 * (1.0 + bend)
        value = gate * half
        slope = half + 0.5 * gate * (1.0 - bend * bend) * (
            0.7978845608 * (1.0 + 3.0 * 0.044715 * square)
        )
        hidden = (value * linear).astype(BF)
        if step == 0:
            pltpu.make_async_copy(down, down, down_sem).wait()
        total = total + matmul(hidden, down[at, :])
        grad_hidden = matmul_nt(grad, down[at, :])
        grad_gate = (grad_hidden * linear * slope).astype(BF)
        grad_linear = (grad_hidden * value).astype(BF)
        grad_normed = grad_normed + (
            matmul_nt(grad_gate, weights[:, at]) + matmul_nt(grad_linear, weights[:, next_at])
        )
        terms[:, at] = matmul_tn(normed, grad_gate).astype(BF)
        save(step, 0).start()
        terms[:, next_at] = matmul_tn(normed, grad_linear).astype(BF)
        save(step, 1).start()
        terms_down[at, :] = matmul_tn(hidden, grad).astype(BF)

    def store_down(group, carry):
        tile_copies(group, 1, terms_ref, terms_down, down_out_sem)
        return carry

    lax.fori_loop(0, inner // deep, store_down, 0)
    out_ref[...] = total.astype(BF)
    part, grad_gain = norm_backward(resid_ref[...], gains_ref[2:3, :], grad_normed)
    grad_resid_ref[...] = grad.astype(F32) + part
    grad_gain_ref[...] = grad_gain
    for step in range(steps):
        for side in range(2):
            save(step, side).wait()
    pltpu.make_async_copy(terms_down, terms_down, down_out_sem).wait()


def cross_backward(per_head, grad_ref, resid_ref, normed_ref, rows_ref, kv_ref, mixed_ref,
                   weights_ref, enc_ref, wa_ref, wb_ref, gains_ref,
                   out_ref, grad_gain_ref, terms_a_ref, terms_b_ref, enc_grad_ref,
                   mix_grad, row_grad, kv_grad):
    rows, width = grad_ref.shape
    low = grad_ref[...].astype(BF)
    mix_grad[...] = matmul_nt(low, wb_ref[:, width:]).astype(BF)
    terms_b_ref[:, width:] = matmul_tn(mixed_ref[...], low).astype(BF)
    for pair in range(width // (2 * per_head)):
        at = pl.ds(pair * 2 * per_head, 2 * per_head)
        value_at = pl.ds(width + pair * 2 * per_head, 2 * per_head)
        row_grad[:, at], kv_grad[:, at], kv_grad[:, value_at], _ = attention_pair_grad(
            rows_ref[:, at], kv_ref[:, at], kv_ref[:, value_at], mixed_ref[:, at], mix_grad[:, at],
            weights_ref[pl.ds(pair * 2 * rows, 2 * rows), :], per_head,
        )
    part, grad_gain = norm_backward(
        resid_ref[...], gains_ref[1:2, :], matmul_nt(row_grad[...], wb_ref[:, :width])
    )
    out_ref[...] = grad_ref[...] + part
    grad_gain_ref[...] = grad_gain
    terms_b_ref[:, :width] = matmul_tn(normed_ref[...], row_grad[...]).astype(BF)
    terms_a_ref[...] = matmul_tn(enc_ref[...], kv_grad[...]).astype(BF)
    enc_grad_ref[...] = matmul_nt(kv_grad[...], wa_ref[...])[: enc_grad_ref.shape[0]]


def self_backward(per_head, grad_ref, x_ref, normed_ref, qkv_ref, mixed_ref, weights_ref,
                  wa_ref, wb_ref, gains_ref,
                  out_ref, grad_gain_ref, terms_a_ref, terms_b_ref, score_ref,
                  mix_grad, qkv_grad):
    rows, width = grad_ref.shape
    low = grad_ref[...].astype(BF)
    mix_grad[...] = matmul_nt(low, wb_ref[:, width:]).astype(BF)
    terms_b_ref[:, width:] = matmul_tn(mixed_ref[...], low).astype(BF)
    for pair in range(width // (2 * per_head)):
        at = pl.ds(pair * 2 * per_head, 2 * per_head)
        key_at = pl.ds(width + pair * 2 * per_head, 2 * per_head)
        value_at = pl.ds(2 * width + pair * 2 * per_head, 2 * per_head)
        here = pl.ds(pair * 2 * rows, 2 * rows)
        qkv_grad[:, at], qkv_grad[:, key_at], qkv_grad[:, value_at], grad_scores = (
            attention_pair_grad(
                qkv_ref[:, at], qkv_ref[:, key_at], qkv_ref[:, value_at], mixed_ref[:, at],
                mix_grad[:, at], weights_ref[here, :], per_head,
            )
        )
        for side in range(2):
            score_ref[pl.ds(2 * pair + side, 1), :] = diagonal_sums(
                grad_scores[side * rows : (side + 1) * rows]
            )
    grad_qk, grad_v = qkv_grad[:, : 2 * width], qkv_grad[:, 2 * width :]
    terms_a_ref[...] = matmul_tn(normed_ref[...], grad_qk).astype(BF)
    terms_b_ref[:, :width] = matmul_tn(normed_ref[...], grad_v).astype(BF)
    cotangent = matmul_nt(grad_qk, wa_ref[:, : 2 * width]) + matmul_nt(grad_v, wb_ref[:, :width])
    part, grad_gain = norm_backward(x_ref[...].astype(F32), gains_ref[0:1, :], cotangent)
    out_ref[...] = grad_ref[...] + part
    grad_gain_ref[...] = grad_gain


def whole(kernel, outs, scratch=()):
    return pl.pallas_call(
        kernel,
        out_shape=[jax.ShapeDtypeStruct(*out) for out in outs],
        scratch_shapes=[pltpu.VMEM(*piece) for piece in scratch],
        compiler_params=pltpu.CompilerParams(vmem_limit_bytes=56 << 20),
    )


def body(
    layer_input, encoder_states, output_grad,
    self_query, self_key, self_value, self_output,
    cross_query, cross_key, cross_value, cross_output,
    feed_gate, feed_up, feed_down,
    gain_self, gain_cross, gain_feed,
    bias_table, target_lengths, source_lengths, distance_bucket, *, count,
):
    width = layer_input.shape[1]
    rows = gain_self.shape[0]
    inner = feed_gate.shape[1]
    block = tile_block(width, inner)
    direct = rows % block == 0
    down_piece = to_tiles(feed_down, block, inner) if direct else feed_down.reshape(rows, -1)
    feed_piece = jnp.concatenate([feed_gate, feed_up, down_piece], axis=1)
    feed_all = lax.all_gather(feed_piece, AXIS, axis=0, tiled=True)
    gains = jnp.stack([gain_self, gain_cross, gain_feed], axis=1)
    gains = jnp.pad(gains, ((0, 0), (0, 128 - gains.shape[1])))
    self_piece = jnp.concatenate([self_query, self_key, gains, self_value, self_output], axis=1)
    cross_piece = jnp.concatenate([cross_key, cross_value, cross_query, cross_output], axis=1)
    self_held = gather_high(self_piece, count)
    self_held, cross_piece = tied(self_held, cross_piece)
    self_a, self_b = gather_last(gather_middle(self_held, 2 * width + 128, count), count)
    cross_halves = gather_middle(gather_high(cross_piece, count), 2 * width, count)
    if not direct:
        down_all = feed_all[:, 2 * inner :].reshape(inner, width)
        feed_all = jnp.concatenate(
            [feed_all[:, : 2 * inner], to_tiles(down_all, block, inner)], axis=1
        )

    row_count = layer_input.shape[0]
    onehot = (
        distance_bucket[:, None] == jnp.arange(bias_table.shape[0], dtype=jnp.int32)[None, :]
    ).astype(F32)
    per_distance = jnp.dot(onehot, bias_table, precision=lax.Precision.HIGHEST)
    bias_rows = jnp.pad(per_distance.T, ((0, 0), (0, row_count - per_distance.shape[0])))
    bias = jax.vmap(toeplitz)(bias_rows)
    target_segment = segment_ids(target_lengths[0], row_count)
    source_count = encoder_states.shape[0]
    source_segment = segment_ids(source_lengths[0], source_count)
    position = jnp.arange(row_count, dtype=jnp.int32)
    causal = (target_segment[:, None] == target_segment[None, :]) & (
        position[None, :] <= position[:, None]
    )
    aligned = target_segment[:, None] == source_segment[None, :]
    masked_bias = jnp.where(causal[None], bias, MASKED).reshape(-1, row_count)
    mask = jnp.pad(
        jnp.where(aligned, 0.0, MASKED), ((0, 0), (0, row_count - source_count)),
        constant_values=MASKED,
    )
    encoder = jnp.pad(encoder_states, ((0, row_count - source_count), (0, 0)))
    per_head = width // H
    low, wide = ((row_count, width), BF), ((row_count, width), F32)
    kept = ((H * row_count, row_count), F32)
    one_row = ((1, width), F32)

    gains, normed_one, qkv, mixed_one, weights_one, resid_one = whole(
        partial(self_forward, per_head),
        (((8, width), F32), low, ((row_count, 3 * width), BF), low, kept, wide),
    )(layer_input, self_a, self_b, masked_bias)
    resid_one, *cross_halves = tied(resid_one, *cross_halves)
    cross_a, cross_b = gather_last(cross_halves, count)
    normed_two, cross_rows, cross_kv, mixed_two, weights_two, resid_two, normed_three = whole(
        partial(cross_forward, per_head),
        (low, low, ((row_count, 2 * width), BF), low, kept, wide, low),
    )(resid_one, encoder, cross_a, cross_b, gains, mask)
    chunk = min(512, inner)
    steps = inner // chunk
    in_vmem, in_hbm = pl.BlockSpec(memory_space=pltpu.VMEM), pl.BlockSpec(memory_space=pl.ANY)
    layer_output, grad_resid_two, grad_gain_feed, terms_feed = pl.pallas_call(
        partial(feed_step, chunk, block),
        out_shape=[
            jax.ShapeDtypeStruct(*o) for o in (low, wide, one_row, ((width, 3 * inner), BF))
        ],
        in_specs=[in_vmem] * 4 + [in_hbm],
        out_specs=[in_vmem] * 3 + [in_hbm],
        scratch_shapes=[
            pltpu.VMEM((width, 2 * inner), BF), pltpu.VMEM((inner, width), BF),
            pltpu.VMEM((width, 2 * inner), BF), pltpu.VMEM((inner, width), BF),
            pltpu.SemaphoreType.DMA((steps, 2)), pltpu.SemaphoreType.DMA,
            pltpu.SemaphoreType.DMA((steps, 2)), pltpu.SemaphoreType.DMA,
        ],
        compiler_params=pltpu.CompilerParams(vmem_limit_bytes=56 << 20),
    )(resid_two, normed_three, output_grad, gains, feed_all)
    if not direct:
        terms_down = from_tiles(terms_feed[:, 2 * inner :], block, width)
        terms_feed = jnp.concatenate(
            [terms_feed[:, : 2 * inner], terms_down.reshape(width, inner)], axis=1
        )
    share_feed = lax.psum_scatter(terms_feed, AXIS, scatter_dimension=0, tiled=True).astype(F32)
    share_gate, share_up = share_feed[:, :inner], share_feed[:, inner : 2 * inner]
    share_down = share_feed[:, 2 * inner :]
    share_down = from_tiles(share_down, block, width) if direct else share_down.reshape(feed_down.shape)
    terms = ((width, 2 * width), BF)
    grad_resid_one, grad_gain_cross, terms_ckv, terms_cqo, encoder_grad = whole(
        partial(cross_backward, per_head),
        (wide, one_row, terms, terms, ((source_count, width), F32)),
        (low, low, ((row_count, 2 * width), BF)),
    )(
        grad_resid_two, resid_one, normed_two, cross_rows, cross_kv, mixed_two, weights_two,
        encoder, cross_a, cross_b, gains,
    )
    cross_sum = Reduction(terms_ckv, terms_cqo, count)
    cross_sum.advance()
    (grad_resid_one,) = cross_sum.tie(grad_resid_one)
    cross_sum.advance()
    input_grad, grad_gain_self, terms_qk, terms_vo, grad_scores = whole(
        partial(self_backward, per_head),
        (wide, one_row, terms, terms, ((H, row_count), F32)),
        (low, ((row_count, 3 * width), BF)),
    )(
        grad_resid_one, layer_input, normed_one, qkv, mixed_one, weights_one,
        self_a, self_b, gains,
    )
    self_sum = Reduction(terms_qk, terms_vo, count)
    self_sum.parts[0], self_sum.parts[1] = cross_sum.tie(*self_sum.parts)
    self_sum.advance()
    share_cross = cross_sum.finish()
    grad_bias_rows = jnp.roll(grad_scores[:, ::-1], 1, axis=1)
    grad_table = jnp.dot(
        onehot.T, grad_bias_rows[:, : onehot.shape[0]].T, precision=lax.Precision.HIGHEST
    )
    table_rows = jnp.pad(grad_table, ((0, 0), (0, width - grad_table.shape[1])))
    small = jnp.concatenate(
        [grad_gain_self, grad_gain_cross, grad_gain_feed, table_rows], axis=0
    )
    small = total_sum(small, count)
    share_self = self_sum.finish()
    own = lax.dynamic_slice_in_dim(small[:3], lax.axis_index(AXIS) * rows, rows, axis=1)
    return (
        layer_output, input_grad, encoder_grad,
        *(share_self[:, i * width : (i + 1) * width] for i in range(4)),
        *(share_cross[:, i * width : (i + 1) * width] for i in (2, 0, 1, 3)),
        share_gate, share_up, share_down,
        own[0], own[1], own[2], small[3:, : grad_table.shape[1]],
    )


def solution(mesh):
    count = mesh.shape[AXIS]
    rows, flat, full = P(AXIS, None), P(AXIS), P()

    def step(*args):
        return body(*args, count=count)

    return jax.shard_map(
        step,
        mesh=mesh,
        in_specs=(rows,) * 14 + (flat,) * 3 + (full, rows, rows, full),
        out_specs=(rows,) * 14 + (flat,) * 3 + (full,),
        check_vma=False,
    )
```

time: 523 us -> 337 us (0.64); the launches traced: 513 us -> 336 us
  starting transfers between devices: 113 us -> 40.7 us
  matrix products: 60.1 us -> 1.21 us
  Pallas kernels: 0 us -> 43.3 us
  local copies, waits for them, and re-layouts: 63 us -> 26.8 us
  waiting for transfers between devices: 227 us -> 192 us
  other arithmetic: 45.7 us -> 16.5 us
  between operations: 3.72 us -> 14.8 us
    ppermute x100 -> x32, waiting for transfers between devices: 217 us -> 132 us  [the longest x16 73.7 us: swap_blocks(): other = lax.ppermute(held, AXIS, partner(count, bit))]
    ppermute x100 -> x32, starting transfers between devices: 102 us -> 39.6 us  [the longest x16 25.5 us: swap_blocks(): other = lax.ppermute(held, AXIS, partner(count, bit))]
    dot_general x42 -> x0, matrix products: 58.9 us -> none  [the longest x10 18.4 us: matmul_tn(): lax.dot_general(left, right, (((0,), (0,)), ((), ())), preferred_element_...]
    pallas_call x0 -> x5, Pallas kernels: none -> 43.3 us  [the longest x1 14.7 us: body(): pl.pallas_call(partial(feed_step, chunk, block), out_shape=[jax.ShapeDtyp...]
    reduce_scatter x0 -> x1, waiting for transfers between devices: none -> 39.3 us  [body(): lax.psum_scatter(terms_feed, AXIS, scatter_dimension=0, tiled=True)]
    ppermute x5, waiting for transfers between devices: 10.3 us -> 21 us  [total_sum(): values = values + lax.ppermute(values, AXIS, partner(count, bit))]
    unnamed x200 -> x55, local copies, waits for them, and re-layouts: 15.6 us -> 5.11 us
    ppermute x5, starting transfers between devices: 10.9 us -> 1.09 us  [total_sum(): values = values + lax.ppermute(values, AXIS, partner(count, bit))]
  transfers between devices with their start and end apart: 105 -> 39, of which waited for: 59 -> 27; matrix products, arithmetic and copies ran while one was open for 18% -> 10% of each run, Pallas kernels for 0% -> 3%
where the time goes in v2:
time: 337 us; the launch traced here: 336 us
  waiting for transfers between devices  192 us (57%)
  Pallas kernels  43.3 us (13%)
  starting transfers between devices  40.7 us (12%)
  local copies, waits for them, and re-layouts  26.8 us (8%)
  other arithmetic  16.5 us (5%)
  between operations  14.8 us (4%)
    ppermute x16, waiting for transfers between devices, swap_blocks(): other = lax.ppermute(held, AXIS, partner(count, bit))  73.7 us
    ppermute x16, waiting for transfers between devices, fold(): got = lax.ppermute(sent, AXIS, partner(count, bit))  58.5 us
    reduce_scatter x1, waiting for transfers between devices, body(): lax.psum_scatter(terms_feed, AXIS, scatter_dimension=0, tiled=True)  39.3 us
    ppermute x16, starting transfers between devices, swap_blocks(): other = lax.ppermute(held, AXIS, partner(count, bit))  25.5 us
    ppermute x5, waiting for transfers between devices, total_sum(): values = values + lax.ppermute(values, AXIS, partner(count, bit))  21 us
    pallas_call x1, Pallas kernels, body(): pl.pallas_call(partial(feed_step, chunk, block), out_shape=[jax.ShapeDtyp...  14.7 us
    ppermute x16, starting transfers between devices, fold(): got = lax.ppermute(sent, AXIS, partner(count, bit))  14.1 us
    pallas_call x1, Pallas kernels, body(): whole(partial(self_backward, per_head), (wide, one_row, terms, terms, ((H...  9.2 us
  transfers between devices with their start and end apart: 39, of which 27 were waited for; matrix products, arithmetic and copies ran while one was open for 10% of the time, Pallas kernels for 3%

profile of v2, /device:TPU:0, one launch (start us, length us, event | category | flops | bytes accessed | tf_op | source)
XLA Modules:
  0.0 336.0 jit_solution(5500900517493546006)
XLA Ops:
  7.3 1.8 pad_maximum_fusion.14
  11.5 4.1 %collective-permute-start = (bf16[1,24,3200]{2,1,0:T(8,128)(2,1)S(1)}, bf16[1,24,3200]{2,1,0:T(8,128)(2,1)S(1)}, u32[]{:S(2)}, u32[]{:S(2)}) collective-permute-start(bf16[1,24,3200]{2,1,0:T(8,128)(2,1)S(1)} %bitcast.326), channel_id=1, source_target_pairs={{0,16},{1,17},{2,18},{3,19},{4,20},{5,21},{6,22},{7,23},{8,24},{9,... | collective-permute-start | bytes 460808 | tf_op jit(solution)/shard_map/ppermute | solution.py:49
  17.8 3.4 %reshape.730 = f32[12,128,255]{2,1,0:T(8,128)} reshape(f32[12,32640]{1,0:T(8,128)S(1)} %slice.107) | data formatting | bytes 3133440 | tf_op jit(solution)/shard_map/vmap()/reshape | solution.py:157
  21.4 1.5 collective-permute-done
  23.8 13.9 %collective-permute-done.1 = bf16[2,24,3200]{2,1,0:T(8,128)(2,1)S(1)} collective-permute-done((bf16[2,24,3200]{2,1,0:T(8,128)(2,1)S(1)}, bf16[2,24,3200]{2,1,0:T(8,128)(2,1)S(1)}, u32[]{:S(2)}, u32[]{:S(2)}) %collective-permute-start.1) | collective-permute-done | bytes 307232 | tf_op jit(solution)/shard_map/ppermute | solution.py:49
  37.8 2.8 collective-permute-start.8
  40.7 1.0 slice_select_fusion
  41.8 1.5 collective-permute-start.5
  43.3 1.5 collective-permute-start.2
  44.8 6.0 %collective-permute-done.8 = bf16[1,24,3072]{2,1,0:T(8,128)(2,1)S(1)} collective-permute-done((bf16[1,24,3072]{2,1,0:T(8,128)(2,1)S(1)}, bf16[1,24,3072]{2,1,0:T(8,128)(2,1)S(1)}, u32[]{:S(2)}, u32[]{:S(2)}) %collective-permute-start.8) | collective-permute-done | bytes 147488 | tf_op jit(solution)/shard_map/ppermute | solution.py:49
  50.8 2.7 collective-permute-start.9
  53.5 3.1 collective-permute-done.5
  56.7 1.5 collective-permute-start.6
  58.3 8.4 %collective-permute-done.9 = bf16[2,24,3072]{2,1,0:T(8,128)(2,1)S(1)} collective-permute-done((bf16[2,24,3072]{2,1,0:T(8,128)(2,1)S(1)}, bf16[2,24,3072]{2,1,0:T(8,128)(2,1)S(1)}, u32[]{:S(2)}, u32[]{:S(2)}) %collective-permute-start.9) | collective-permute-done | bytes 294944 | tf_op jit(solution)/shard_map/ppermute | solution.py:49
  66.8 1.5 collective-permute-start.10
  68.3 1.5 collective-permute-start.12
  70.6 11.1 %collective-permute-done.10 = bf16[4,24,1536]{2,1,0:T(8,128)(2,1)S(1)} collective-permute-done((bf16[4,24,1536]{2,1,0:T(8,128)(2,1)S(1)}, bf16[4,24,1536]{2,1,0:T(8,128)(2,1)S(1)}, u32[]{:S(2)}, u32[]{:S(2)}) %collective-permute-start.10) | collective-permute-done | bytes 294944 | tf_op jit(solution)/shard_map/ppermute | solution.py:49
  81.7 1.7 collective-permute-done.12
  83.8 5.7 %collective-permute-start.11 = (bf16[8,24,1536]{2,1,0:T(8,128)(2,1)S(1)}, bf16[8,24,1536]{2,1,0:T(8,128)(2,1)S(1)}, u32[]{:S(2)}, u32[]{:S(2)}) collective-permute-start(bf16[8,24,1536]{2,1,0:T(8,128)(2,1)S(1)} %bitcast.304), channel_id=1, source_target_pairs={{0,2},{1,3},{2,0},{3,1},{4,6},{5,7},{6,4},{7,5},{8,10},{9,11},{10,... | collective-permute-start | bytes 1769480 | tf_op jit(solution)/shard_map/ppermute | solution.py:49
  89.5 19.3 %collective-permute-done.3 = bf16[8,24,1664]{2,1,0:T(8,128)(2,1)S(1)} collective-permute-done((bf16[8,24,1664]{2,1,0:T(8,128)(2,1)S(1)}, bf16[8,24,1664]{2,1,0:T(8,128)(2,1)S(1)}, u32[]{:S(2)}, u32[]{:S(2)}) %collective-permute-start.3) | collective-permute-done | bytes 639008 | tf_op jit(solution)/shard_map/ppermute | solution.py:49
  110.2 8.9 %collective-permute-done.11 = bf16[8,24,1536]{2,1,0:T(8,128)(2,1)S(1)} collective-permute-done((bf16[8,24,1536]{2,1,0:T(8,128)(2,1)S(1)}, bf16[8,24,1536]{2,1,0:T(8,128)(2,1)S(1)}, u32[]{:S(2)}, u32[]{:S(2)}) %collective-permute-start.11) | collective-permute-done | bytes 589856 | tf_op jit(solution)/shard_map/ppermute | solution.py:49
  120.3 1.7 copy.183
  122.5 1.7 copy.188
  124.2 5.4 %shard_map.340 = (f32[8,768]{1,0:T(8,128)}, bf16[128,768]{1,0:T(8,128)(2,1)}, bf16[128,2304]{1,0:T(8,128)(2,1)}, bf16[128,768]{1,0:T(8,128)(2,1)}, f32[1536,128]{1,0:T(8,128)}, /*index=5*/f32[128,768]{1,0:T(8,128)}) custom-call(bf16[128,768]{1,0:T(8,128)(2,1)} %x_ref.3, bf16[768,1664]{1,0:T(8,128)(2,1)} %bitcast.264, bf16[768,1536]{1,0:T(8,128)(2,1)} %bitcast.270, ...), custom_call_target="tpu_custom_call" | custom-call | tf_op jit(solution)/shard_map/pallas_call | solution.py:519
  130.3 1.6 pad.23.enc_ref
  132.6 1.4 select_bitcast_fusion.3
  134.3 1.7 copy.199
  136.3 1.7 copy.198
  138.1 5.7 %shard_map.341 = (bf16[128,768]{1,0:T(8,128)(2,1)}, bf16[128,768]{1,0:T(8,128)(2,1)}, bf16[128,1536]{1,0:T(8,128)(2,1)}, bf16[128,768]{1,0:T(8,128)(2,1)}, f32[1...) custom-call(f32[128,768]{1,0:T(8,128)} %get-tuple-element.60.resid_ref, ...), custom_call_target="tpu_custom_call" | custom-call | tf_op jit(solution)/shard_map/pallas_call | solution.py:525
  143.7 14.7 %shard_map.342 = (bf16[128,768]{1,0:T(8,128)(2,1)}, f32[128,768]{1,0:T(8,128)}, f32[1,768]{1,0:T(1,128)}, bf16[768,6144]{1,0:T(8,128)(2,1)}) custom-call(f32[128,768]{1,0:T(8,128)} %get-tuple-element.64.resid_ref, bf16[128,768]{1,0:T(8,128)(2,1)} %get-tuple-element.65.normed_ref, bf16[128,768]{1,0:T(8,128)(2,1)} %grad_ref.1, ...), custom_call_target="tpu_custom_call" | custom-call | tf_op jit(solution)/shard_map/pallas_call | solution.py:532
  158.5 8.3 %shard_map.343 = (f32[128,768]{1,0:T(8,128)}, f32[1,768]{1,0:T(1,128)}, bf16[768,1536]{1,0:T(8,128)(2,1)}, bf16[768,1536]{1,0:T(8,128)(2,1)}, f32[64,768]{1,0:T(8,128)}) custom-call(f32[128,768]{1,0:T(8,128)} %get-tuple-element.67.grad_ref, f32[128,768]{1,0:T(8,128)} %get-tuple-element.60.resid_ref, bf16[128,768]{1,0:T(8,128)(2,1)} %get-tuple-element.68.normed_ref, ...), custom_call_target="tpu_custom_call" | custom-call | tf_op jit(solution)/shard_map/pallas_call | solution.py:557
  166.8 1.5 dynamic-slice_bitcast_fusion.2
  168.8 1.1 dynamic-slice_bitcast_fusion.3
  170.0 1.4 collective-permute-done.17
  171.3 1.6 fusion.5
  173.1 1.6 fusion.4
  174.7 9.2 %shard_map.344 = (f32[128,768]{1,0:T(8,128)}, f32[1,768]{1,0:T(1,128)}, bf16[768,1536]{1,0:T(8,128)(2,1)}, bf16[768,1536]{1,0:T(8,128)(2,1)}, f32[12,128]{1,0:T(8,128)}) custom-call(f32[128,768]{1,0:T(8,128)} %get-tuple-element.76.grad_ref, bf16[128,768]{1,0:T(8,128)(2,1)} %x_ref.3, bf16[128,768]{1,0:T(8,128)(2,1)} %get-tuple-element.77.normed_ref, ...), custom_call_target="tpu_custom_call" | custom-call | tf_op jit(solution)/shard_map/pallas_call | solution.py:569
  184.8 1.0 fusion.30
  186.7 1.2 collective-permute-done.32
  188.3 1.8 collective-permute-start.19
  190.1 4.1 %collective-permute-done.33 = f32[35,768]{1,0:T(8,128)S(1)} collective-permute-done((f32[35,768]{1,0:T(8,128)S(1)}, f32[35,768]{1,0:T(8,128)S(1)}, u32[]{:S(2)}, u32[]{:S(2)}) %collective-permute-start.33) | collective-permute-done | bytes 107552 | tf_op jit(solution)/shard_map/ppermute | solution.py:137
  194.6 4.5 %collective-permute-done.34 = f32[35,768]{1,0:T(8,128)S(1)} collective-permute-done((f32[35,768]{1,0:T(8,128)S(1)}, f32[35,768]{1,0:T(8,128)S(1)}, u32[]{:S(2)}, u32[]{:S(2)}) %collective-permute-start.34) | collective-permute-done | bytes 107552 | tf_op jit(solution)/shard_map/ppermute | solution.py:137
  199.8 5.2 %collective-permute-done.35 = f32[35,768]{1,0:T(8,128)} collective-permute-done((f32[35,768]{1,0:T(8,128)}, f32[35,768]{1,0:T(8,128)}, u32[]{:S(2)}, u32[]{:S(2)}) %collective-permute-start.35) | collective-permute-done | bytes 107552 | tf_op jit(solution)/shard_map/ppermute | solution.py:137
  205.0 1.0 add.172
  206.5 6.1 %collective-permute-done.36 = f32[35,768]{1,0:T(8,128)S(1)} collective-permute-done((f32[35,768]{1,0:T(8,128)S(1)}, f32[35,768]{1,0:T(8,128)S(1)}, u32[]{:S(2)}, u32[]{:S(2)}) %collective-permute-start.36) | collective-permute-done | bytes 107552 | tf_op jit(solution)/shard_map/ppermute | solution.py:137
  212.9 6.5 %collective-permute-done.18 = bf16[4,2,24,1536]{3,2,1,0:T(8,128)(2,1)S(1)} collective-permute-done((bf16[4,2,24,1536]{3,2,1,0:T(8,128)(2,1)S(1)}, bf16[4,2,24,1536]{3,2,1,0:T(8,128)(2,1)S(1)}, u32[]{:S(2)}, u32[]{:S(2)}) %collective-permute-start.18) | collective-permute-done | bytes 589856 | tf_op jit(solution)/shard_map/ppermute | solution.py:94
  221.3 1.7 collective-permute-start.28
  223.0 3.4 %collective-permute-done.29 = bf16[4,1,24,1536]{3,2,0,1:T(8,128)(2,1)S(1)} collective-permute-done((bf16[4,1,24,1536]{3,2,0,1:T(8,128)(2,1)S(1)}, bf16[4,1,24,1536]{3,2,0,1:T(8,128)(2,1)S(1)}, u32[]{:S(2)}, u32[]{:S(2)}) %collective-permute-start.29) | collective-permute-done | bytes 294944 | tf_op jit(solution)/shard_map/ppermute | solution.py:94
  226.5 1.6 collective-permute-done.28
  228.5 1.5 copy-done.3
  230.1 6.4 %collective-permute-done.30 = bf16[2,1,24,3072]{3,2,0,1:T(8,128)(2,1)S(1)} collective-permute-done((bf16[2,1,24,3072]{3,2,0,1:T(8,128)(2,1)S(1)}, bf16[2,1,24,3072]{3,2,0,1:T(8,128)(2,1)S(1)}, u32[]{:S(2)}, u32[]{:S(2)}) %collective-permute-start.30) | collective-permute-done | bytes 294944 | tf_op jit(solution)/shard_map/ppermute | solution.py:94
  236.6 2.7 collective-permute-start.31
  239.8 1.7 collective-permute-start.24
  242.3 15.2 %collective-permute-done.24 = bf16[8,1,24,1536]{3,2,0,1:T(8,128)(2,1)S(1)} collective-permute-done((bf16[8,1,24,1536]{3,2,0,1:T(8,128)(2,1)S(1)}, bf16[8,1,24,1536]{3,2,0,1:T(8,128)(2,1)S(1)}, u32[]{:S(2)}, u32[]{:S(2)}) %collective-permute-start.24) | collective-permute-done | bytes 589856 | tf_op jit(solution)/shard_map/ppermute | solution.py:94
  257.7 1.7 collective-permute-start.25
  259.4 1.3 collective-permute-done.21
  261.0 5.4 %collective-permute-done.25 = bf16[4,1,24,1536]{3,2,0,1:T(8,128)(2,1)S(1)} collective-permute-done((bf16[4,1,24,1536]{3,2,0,1:T(8,128)(2,1)S(1)}, bf16[4,1,24,1536]{3,2,0,1:T(8,128)(2,1)S(1)}, u32[]{:S(2)}, u32[]{:S(2)}) %collective-permute-start.25) | collective-permute-done | bytes 294944 | tf_op jit(solution)/shard_map/ppermute | solution.py:94
  266.5 5.2 %collective-permute-done.22 = bf16[4,1,24,1536]{3,2,1,0:T(8,128)(2,1)S(1)} collective-permute-done((bf16[4,1,24,1536]{3,2,1,0:T(8,128)(2,1)S(1)}, bf16[4,1,24,1536]{3,2,1,0:T(8,128)(2,1)S(1)}, u32[]{:S(2)}, u32[]{:S(2)}) %collective-permute-start.22) | collective-permute-done | bytes 294944 | tf_op jit(solution)/shard_map/ppermute | solution.py:94
  271.8 0.9 collective-permute-start.26
  272.7 6.8 %collective-permute-done.26 = bf16[2,1,24,3072]{3,2,0,1:T(8,128)(2,1)S(1)} collective-permute-done((bf16[2,1,24,3072]{3,2,0,1:T(8,128)(2,1)S(1)}, bf16[2,1,24,3072]{3,2,0,1:T(8,128)(2,1)S(1)}, u32[]{:S(2)}, u32[]{:S(2)}) %collective-permute-start.26) | collective-permute-done | bytes 294944 | tf_op jit(solution)/shard_map/ppermute | solution.py:94
  279.6 1.8 collective-permute-start.27
  282.1 5.2 %collective-permute-done.27 = bf16[1,1,24,3072]{3,2,0,1:T(8,128)(2,1)S(1)} collective-permute-done((bf16[1,1,24,3072]{3,2,0,1:T(8,128)(2,1)S(1)}, bf16[1,1,24,3072]{3,2,0,1:T(8,128)(2,1)S(1)}, u32[]{:S(2)}, u32[]{:S(2)}) %collective-permute-start.27) | collective-permute-done | bytes 147488 | tf_op jit(solution)/shard_map/ppermute | solution.py:94
  288.0 39.3 %reduce-scatter.2.cloned.1.call-done = bf16[24,6144]{1,0:T(8,128)(2,1)} async-done(((bf16[768,6144]{1,0:T(8,128)(2,1)}), bf16[24,6144]{1,0:T(8,128)(2,1)}) %reduce-scatter.2.cloned.1.call-update) | async-done | bytes 294928 | tf_op jit(solution)/shard_map/reduce_scatter | solution.py:552
  327.3 1.8 fusion.40
  (192 shorter events, 23.4 us)
Async XLA Ops:
  7.2 8.7 %copy-start = (f32[32,12]{0,1:T(8,128)S(1)}, f32[32,12]{0,1:T(8,128)}, u32[]{:S(2)}) copy-start(f32[32,12]{0,1:T(8,128)} %param.38) | copy-start | bytes 4612
  7.2 4.3 %copy-start.10 = (bf16[24,768]{1,0:T(8,128)(2,1)S(1)}, bf16[24,768]{1,0:T(8,128)(2,1)}, u32[]{:S(2)}) copy-start(bf16[24,768]{1,0:T(8,128)(2,1)} %param.26) | copy-start | bytes 110596
  7.2 4.3 %copy-start.11 = (bf16[24,768]{1,0:T(8,128)(2,1)S(1)}, bf16[24,768]{1,0:T(8,128)(2,1)}, u32[]{:S(2)}) copy-start(bf16[24,768]{1,0:T(8,128)(2,1)} %param.27) | copy-start | bytes 110596
  7.2 8.5 %copy-start.19 = (s32[1,4]{1,0:T(1,128)S(1)}, s32[1,4]{1,0:T(1,128)}, u32[]{:S(2)}) copy-start(s32[1,4]{1,0:T(1,128)} %param.39) | copy-start | bytes 52
  7.2 8.7 %copy-start.21 = (s32[80]{0:T(128)S(1)}, s32[80]{0:T(128)}, u32[]{:S(2)}) copy-start(s32[80]{0:T(128)} %param.41) | copy-start | bytes 964
  7.2 136.5 %all-gather.2.cloned.1.call-start = ((), (), s32[]{:S(2)}) async-start(), calls=%async_computation.1 | async-start | bytes 9732096 | tf_op jit(solution)/shard_map/all_gather | solution.py:478
  9.1 318.2 %reduce-scatter.2.cloned.1.call-start = ((), (), s32[]{:S(2)}) async-start(), calls=%async_computation.2 | async-start | bytes 9732096 | tf_op jit(solution)/shard_map/reduce_scatter | solution.py:552
  11.5 11.4 %collective-permute-start = (bf16[1,24,3200]{2,1,0:T(8,128)(2,1)S(1)}, bf16[1,24,3200]{2,1,0:T(8,128)(2,1)S(1)}, u32[]{:S(2)}, u32[]{:S(2)}) collective-permute-start(bf16[1,24,3200]{2,1,0:T(8,128)(2,1)S(1)} %bitcast.326), channel_id=1, source_target_pairs={{0,16},{1,17},{2,18},{3,19},{4,20},{5,21},{6,22},{7,23},{8,24},{9,... | collective-permute-start | bytes 460808 | tf_op jit(solution)/shard_map/ppermute | solution.py:49
  17.8 3.4 %copy-start.8 = (bf16[24,768]{1,0:T(8,128)(2,1)S(1)}, bf16[24,768]{1,0:T(8,128)(2,1)}, u32[]{:S(2)}) copy-start(bf16[24,768]{1,0:T(8,128)(2,1)} %param.24) | copy-start | bytes 110596
  17.8 3.4 %copy-start.9 = (bf16[24,768]{1,0:T(8,128)(2,1)S(1)}, bf16[24,768]{1,0:T(8,128)(2,1)}, u32[]{:S(2)}) copy-start(bf16[24,768]{1,0:T(8,128)(2,1)} %param.25) | copy-start | bytes 110596
  21.2 2.6 copy-start.12
  21.2 2.6 copy-start.13
  21.2 2.6 copy-start.14
  21.2 2.6 copy-start.15
  23.0 14.7 %collective-permute-start.1 = (bf16[2,24,3200]{2,1,0:T(8,128)(2,1)S(1)}, bf16[2,24,3200]{2,1,0:T(8,128)(2,1)S(1)}, u32[]{:S(2)}, u32[]{:S(2)}) collective-permute-start(bf16[2,24,3200]{2,1,0:T(8,128)(2,1)S(1)} %maximum_bitcast_fusion), channel_id=1, source_target_pairs={{0,8},{1,9},{2,10},{3,11},{4,12},{5,13},{6,14},{7,15},{8,0},{9,1},... | collective-permute-start | bytes 921608 | tf_op jit(solution)/shard_map/ppermute | solution.py:49
  23.8 16.9 %copy-start.2 = (f32[12,128,255]{2,1,0:T(8,128)S(1)}, f32[12,128,255]{2,1,0:T(8,128)}, u32[]{:S(2)}) copy-start(f32[12,128,255]{2,1,0:T(8,128)} %reshape.730) | copy-start | bytes 4700164
  37.8 12.9 %collective-permute-start.8 = (bf16[1,24,3072]{2,1,0:T(8,128)(2,1)S(1)}, bf16[1,24,3072]{2,1,0:T(8,128)(2,1)S(1)}, u32[]{:S(2)}, u32[]{:S(2)}) collective-permute-start(bf16[1,24,3072]{2,1,0:T(8,128)(2,1)S(1)} %bitcast.323), channel_id=1, source_target_pairs={{0,16},{1,17},{2,18},{3,19},{4,20},{5,21},{6,22},{7,23},{8,24},{9,... | collective-permute-start | bytes 442376 | tf_op jit(solution)/shard_map/ppermute | solution.py:49
  41.8 14.8 %collective-permute-start.5 = (bf16[4,24,1536]{2,1,0:T(8,128)(2,1)S(1)}, bf16[4,24,1536]{2,1,0:T(8,128)(2,1)S(1)}, u32[]{:S(2)}, u32[]{:S(2)}) collective-permute-start(bf16[4,24,1536]{2,1,0:T(8,128)(2,1)S(1)} %slice.82), channel_id=1, source_target_pairs={{0,2},{1,3},{2,0},{3,1},{4,6},{5,7},{6,4},{7,5},{8,10},{9,11},{10,... | collective-permute-start | bytes 884744 | tf_op jit(solution)/shard_map/ppermute | solution.py:49
  43.3 26.5 %collective-permute-start.2 = (bf16[4,24,1664]{2,1,0:T(8,128)(2,1)S(1)}, bf16[4,24,1664]{2,1,0:T(8,128)(2,1)S(1)}, u32[]{:S(2)}, u32[]{:S(2)}) collective-permute-start(bf16[4,24,1664]{2,1,0:T(8,128)(2,1)S(1)} %slice.81), channel_id=1, source_target_pairs={{0,4},{1,5},{2,6},{3,7},{4,0},{5,1},{6,2},{7,3},{8,12},{9,13},{10,... | collective-permute-start | bytes 958472 | tf_op jit(solution)/shard_map/ppermute | solution.py:49
  50.8 15.8 %collective-permute-start.9 = (bf16[2,24,3072]{2,1,0:T(8,128)(2,1)S(1)}, bf16[2,24,3072]{2,1,0:T(8,128)(2,1)S(1)}, u32[]{:S(2)}, u32[]{:S(2)}) collective-permute-start(bf16[2,24,3072]{2,1,0:T(8,128)(2,1)S(1)} %maximum_bitcast_fusion.1), channel_id=1, source_target_pairs={{0,8},{1,9},{2,10},{3,11},{4,12},{5,13},{6,14},{7,15},{8,0},{9,1},... | collective-permute-start | bytes 884744 | tf_op jit(solution)/shard_map/ppermute | solution.py:49
  56.7 52.5 %collective-permute-start.6 = (bf16[8,24,1536]{2,1,0:T(8,128)(2,1)S(1)}, bf16[8,24,1536]{2,1,0:T(8,128)(2,1)S(1)}, u32[]{:S(2)}, u32[]{:S(2)}) collective-permute-start(bf16[8,24,1536]{2,1,0:T(8,128)(2,1)S(1)} %bitcast.321), channel_id=1, source_target_pairs={{0,4},{1,5},{2,6},{3,7},{4,0},{5,1},{6,2},{7,3},{8,12},{9,13},{10,... | collective-permute-start | bytes 1769480 | tf_op jit(solution)/shard_map/ppermute | solution.py:49
  66.8 14.9 %collective-permute-start.10 = (bf16[4,24,1536]{2,1,0:T(8,128)(2,1)S(1)}, bf16[4,24,1536]{2,1,0:T(8,128)(2,1)S(1)}, u32[]{:S(2)}, u32[]{:S(2)}) collective-permute-start(bf16[4,24,1536]{2,1,0:T(8,128)(2,1)S(1)} %get-tuple-element.161), channel_id=1, source_target_pairs={{0,4},{1,5},{2,6},{3,7},{4,0},{5,1},{6,2},{7,3},{8,12},{9,13},{10,... | collective-permute-start | bytes 884744 | tf_op jit(solution)/shard_map/ppermute | solution.py:49
  68.3 15.0 %collective-permute-start.12 = (bf16[4,24,1536]{2,1,0:T(8,128)(2,1)S(1)}, bf16[4,24,1536]{2,1,0:T(8,128)(2,1)S(1)}, u32[]{:S(2)}, u32[]{:S(2)}) collective-permute-start(bf16[4,24,1536]{2,1,0:T(8,128)(2,1)S(1)} %get-tuple-element.160), channel_id=1, source_target_pairs={{0,2},{1,3},{2,0},{3,1},{4,6},{5,7},{6,4},{7,5},{8,10},{9,11},{10,... | collective-permute-start | bytes 884744 | tf_op jit(solution)/shard_map/ppermute | solution.py:49
  70.0 38.7 %collective-permute-start.3 = (bf16[8,24,1664]{2,1,0:T(8,128)(2,1)S(1)}, bf16[8,24,1664]{2,1,0:T(8,128)(2,1)S(1)}, u32[]{:S(2)}, u32[]{:S(2)}) collective-permute-start(bf16[8,24,1664]{2,1,0:T(8,128)(2,1)S(1)} %bitcast.303), channel_id=1, source_target_pairs={{0,2},{1,3},{2,0},{3,1},{4,6},{5,7},{6,4},{7,5},{8,10},{9,11},{10,... | collective-permute-start | bytes 1916936 | tf_op jit(solution)/shard_map/ppermute | solution.py:49
  83.6 25.7 %collective-permute-start.13 = (bf16[8,24,1536]{2,1,0:T(8,128)(2,1)S(1)}, bf16[8,24,1536]{2,1,0:T(8,128)(2,1)S(1)}, u32[]{:S(2)}, u32[]{:S(2)}) collective-permute-start(bf16[8,24,1536]{2,1,0:T(8,128)(2,1)S(1)} %bitcast.322), channel_id=1, source_target_pairs={{0,4},{1,5},{2,6},{3,7},{4,0},{5,1},{6,2},{7,3},{8,12},{9,13},{10,... | collective-permute-start | bytes 1769480 | tf_op jit(solution)/shard_map/ppermute | solution.py:49
  83.8 35.3 %collective-permute-start.11 = (bf16[8,24,1536]{2,1,0:T(8,128)(2,1)S(1)}, bf16[8,24,1536]{2,1,0:T(8,128)(2,1)S(1)}, u32[]{:S(2)}, u32[]{:S(2)}) collective-permute-start(bf16[8,24,1536]{2,1,0:T(8,128)(2,1)S(1)} %bitcast.304), channel_id=1, source_target_pairs={{0,2},{1,3},{2,0},{3,1},{4,6},{5,7},{6,4},{7,5},{8,10},{9,11},{10,... | collective-permute-start | bytes 1769480 | tf_op jit(solution)/shard_map/ppermute | solution.py:49
  109.2 10.5 %collective-permute-start.4 = (bf16[16,24,1664]{2,1,0:T(8,128)(2,1)S(1)}, bf16[16,24,1664]{2,1,0:T(8,128)(2,1)S(1)}, u32[]{:S(2)}, u32[]{:S(2)}) collective-permute-start(bf16[16,24,1664]{2,1,0:T(8,128)(2,1)S(1)} %bitcast.280), channel_id=1, source_target_pairs={{0,1},{1,0},{2,3},{3,2},{4,5},{5,4},{6,7},{7,6},{8,9},{9,8},{10,11... | collective-permute-start | bytes 3833864 | tf_op jit(solution)/shard_map/ppermute | solution.py:49
  109.7 12.3 %collective-permute-start.7 = (bf16[16,24,1536]{2,1,0:T(8,128)(2,1)S(1)}, bf16[16,24,1536]{2,1,0:T(8,128)(2,1)S(1)}, u32[]{:S(2)}, u32[]{:S(2)}) collective-permute-start(bf16[16,24,1536]{2,1,0:T(8,128)(2,1)S(1)} %bitcast.285), channel_id=1, source_target_pairs={{0,1},{1,0},{2,3},{3,2},{4,5},{5,4},{6,7},{7,6},{8,9},{9,8},{10,11... | collective-permute-start | bytes 3538952 | tf_op jit(solution)/shard_map/ppermute | solution.py:49
  124.2 5.4 %copy-start.20 = (s32[1,4]{1,0:T(1,128)S(1)}, s32[1,4]{1,0:T(1,128)}, u32[]{:S(2)}) copy-start(s32[1,4]{1,0:T(1,128)} %param.40) | copy-start | bytes 52
  129.5 3.1 collective-permute-start.15
  129.7 6.2 %collective-permute-start.14 = (bf16[16,24,1536]{2,1,0:T(8,128)(2,1)S(1)}, bf16[16,24,1536]{2,1,0:T(8,128)(2,1)S(1)}, u32[]{:S(2)}, u32[]{:S(2)}) collective-permute-start(bf16[16,24,1536]{2,1,0:T(8,128)(2,1)S(1)} %bitcast.281), channel_id=1, source_target_pairs={{0,1},{1,0},{2,3},{3,2},{4,5},{5,4},{6,7},{7,6},{8,9},{9,8},{10,11... | collective-permute-start | bytes 3538952 | tf_op jit(solution)/shard_map/ppermute | solution.py:49
  166.8 2.0 copy-start.5
  168.3 3.0 collective-permute-start.17
  168.8 2.5 copy-start.7
  169.9 3.2 collective-permute-start.16
  170.0 3.1 copy-start.6
  174.7 11.0 %copy-start.16 = (f32[1,768]{1,0:T(1,128)S(1)}, f32[1,768]{1,0:T(1,128)}, u32[]{:S(2)}) copy-start(f32[1,768]{1,0:T(1,128)} %get-tuple-element.94) | copy-start | bytes 9220
  174.7 11.0 %copy-start.17 = (f32[1,768]{1,0:T(1,128)S(1)}, f32[1,768]{1,0:T(1,128)}, u32[]{:S(2)}) copy-start(f32[1,768]{1,0:T(1,128)} %get-tuple-element.93) | copy-start | bytes 9220
  186.5 1.4 collective-permute-start.32
  186.7 1.2 copy-start.18
  187.9 6.3 %collective-permute-start.33 = (f32[35,768]{1,0:T(8,128)S(1)}, f32[35,768]{1,0:T(8,128)S(1)}, u32[]{:S(2)}, u32[]{:S(2)}) collective-permute-start(f32[35,768]{1,0:T(8,128)S(1)} %fusion.37), channel_id=1, source_target_pairs={{0,2},{1,3},{2,0},{3,1},{4,6},{5,7},{6,4},{7,5},{8,10},{9,11},{10,... | collective-permute-start | bytes 322568 | tf_op jit(solution)/shard_map/ppermute | solution.py:137
  188.3 24.4 %collective-permute-start.19 = (bf16[8,1,24,1536]{3,2,0,1:T(8,128)(2,1)S(1)}, bf16[8,1,24,1536]{3,2,0,1:T(8,128)(2,1)S(1)}, u32[]{:S(2)}, u32[]{:S(2)}) collective-permute-start(bf16[8,1,24,1536]{3,2,0,1:T(8,128)(2,1)S(1)} %dynamic-slice_bitcast_fusion.6), channel_id=1, source_target_pairs={{0,2},{1,3},{2,0},{3,1},{4,6},{5,7},{6,4},{7,5},{8,10},{9,11},{10,... | collective-permute-start | bytes 1769480 | tf_op jit(solution)/shard_map/ppermute | solution.py:94
  194.2 4.9 %collective-permute-start.34 = (f32[35,768]{1,0:T(8,128)S(1)}, f32[35,768]{1,0:T(8,128)S(1)}, u32[]{:S(2)}, u32[]{:S(2)}) collective-permute-start(f32[35,768]{1,0:T(8,128)S(1)} %add.170), channel_id=1, source_target_pairs={{0,4},{1,5},{2,6},{3,7},{4,0},{5,1},{6,2},{7,3},{8,12},{9,13},{10,... | collective-permute-start | bytes 322568 | tf_op jit(solution)/shard_map/ppermute | solution.py:137
  199.8 5.2 %collective-permute-start.35 = (f32[35,768]{1,0:T(8,128)}, f32[35,768]{1,0:T(8,128)}, u32[]{:S(2)}, u32[]{:S(2)}) collective-permute-start(f32[35,768]{1,0:T(8,128)} %add.171), channel_id=1, source_target_pairs={{0,8},{1,9},{2,10},{3,11},{4,12},{5,13},{6,14},{7,15},{8,0},{9,1},... | collective-permute-start | bytes 322568 | tf_op jit(solution)/shard_map/ppermute | solution.py:137
  206.0 6.6 %collective-permute-start.36 = (f32[35,768]{1,0:T(8,128)S(1)}, f32[35,768]{1,0:T(8,128)S(1)}, u32[]{:S(2)}, u32[]{:S(2)}) collective-permute-start(f32[35,768]{1,0:T(8,128)S(1)} %add.172), channel_id=1, source_target_pairs={{0,16},{1,17},{2,18},{3,19},{4,20},{5,21},{6,22},{7,23},{8,24},{9,... | collective-permute-start | bytes 322568 | tf_op jit(solution)/shard_map/ppermute | solution.py:137
  206.1 13.3 %collective-permute-start.18 = (bf16[4,2,24,1536]{3,2,1,0:T(8,128)(2,1)S(1)}, bf16[4,2,24,1536]{3,2,1,0:T(8,128)(2,1)S(1)}, u32[]{:S(2)}, u32[]{:S(2)}) collective-permute-start(bf16[4,2,24,1536]{3,2,1,0:T(8,128)(2,1)S(1)} %dynamic-slice_bitcast_fusion.7), channel_id=1, source_target_pairs={{0,4},{1,5},{2,6},{3,7},{4,0},{5,1},{6,2},{7,3},{8,12},{9,13},{10,... | collective-permute-start | bytes 1769480 | tf_op jit(solution)/shard_map/ppermute | solution.py:94
  219.6 6.8 %collective-permute-start.29 = (bf16[4,1,24,1536]{3,2,0,1:T(8,128)(2,1)S(1)}, bf16[4,1,24,1536]{3,2,0,1:T(8,128)(2,1)S(1)}, u32[]{:S(2)}, u32[]{:S(2)}) collective-permute-start(bf16[4,1,24,1536]{3,2,0,1:T(8,128)(2,1)S(1)} %dynamic-slice_bitcast_fusion.8), channel_id=1, source_target_pairs={{0,4},{1,5},{2,6},{3,7},{4,0},{5,1},{6,2},{7,3},{8,12},{9,13},{10,... | collective-permute-start | bytes 884744 | tf_op jit(solution)/shard_map/ppermute | solution.py:94
  221.3 7.0 %copy-start.4 = (bf16[768,1536]{1,0:T(8,128)(2,1)S(1)}, bf16[768,1536]{1,0:T(8,128)(2,1)}, u32[]{:S(2)}) copy-start(bf16[768,1536]{1,0:T(8,128)(2,1)} %get-tuple-element.86) | copy-start | bytes 7077892
  221.3 6.8 %collective-permute-start.28 = (bf16[4,1,24,1536]{3,2,0,1:T(8,128)(2,1)S(1)}, bf16[4,1,24,1536]{3,2,0,1:T(8,128)(2,1)S(1)}, u32[]{:S(2)}, u32[]{:S(2)}) collective-permute-start(bf16[4,1,24,1536]{3,2,0,1:T(8,128)(2,1)S(1)} %dynamic-slice_bitcast_fusion.9), channel_id=1, source_target_pairs={{0,2},{1,3},{2,0},{3,1},{4,6},{5,7},{6,4},{7,5},{8,10},{9,11},{10,... | collective-permute-start | bytes 884744 | tf_op jit(solution)/shard_map/ppermute | solution.py:94
  228.2 8.4 %collective-permute-start.30 = (bf16[2,1,24,3072]{3,2,0,1:T(8,128)(2,1)S(1)}, bf16[2,1,24,3072]{3,2,0,1:T(8,128)(2,1)S(1)}, u32[]{:S(2)}, u32[]{:S(2)}) collective-permute-start(bf16[2,1,24,3072]{3,2,0,1:T(8,128)(2,1)S(1)} %fusion.17), channel_id=1, source_target_pairs={{0,8},{1,9},{2,10},{3,11},{4,12},{5,13},{6,14},{7,15},{8,0},{9,1},... | collective-permute-start | bytes 884744 | tf_op jit(solution)/shard_map/ppermute | solution.py:94
  228.3 1.7 copy-start.3
  228.4 11.0 %collective-permute-start.23 = (bf16[16,1,24,1536]{3,2,0,1:T(8,128)(2,1)S(1)}, bf16[16,1,24,1536]{3,2,0,1:T(8,128)(2,1)S(1)}, u32[]{:S(2)}, u32[]{:S(2)}) collective-permute-start(bf16[16,1,24,1536]{3,2,0,1:T(8,128)(2,1)S(1)} %dynamic-slice_bitcast_fusion), channel_id=1, source_target_pairs={{0,1},{1,0},{2,3},{3,2},{4,5},{5,4},{6,7},{7,6},{8,9},{9,8},{10,11... | collective-permute-start | bytes 3538952 | tf_op jit(solution)/shard_map/ppermute | solution.py:94
  230.0 11.4 %collective-permute-start.20 = (bf16[16,1,24,1536]{3,2,0,1:T(8,128)(2,1)S(1)}, bf16[16,1,24,1536]{3,2,0,1:T(8,128)(2,1)S(1)}, u32[]{:S(2)}, u32[]{:S(2)}) collective-permute-start(bf16[16,1,24,1536]{3,2,0,1:T(8,128)(2,1)S(1)} %dynamic-slice_bitcast_fusion.1), channel_id=1, source_target_pairs={{0,1},{1,0},{2,3},{3,2},{4,5},{5,4},{6,7},{7,6},{8,9},{9,8},{10,11... | collective-permute-start | bytes 3538952 | tf_op jit(solution)/shard_map/ppermute | solution.py:94
  236.6 36.0 %collective-permute-start.31 = (bf16[1,1,24,3072]{3,2,0,1:T(8,128)(2,1)S(1)}, bf16[1,1,24,3072]{3,2,0,1:T(8,128)(2,1)S(1)}, u32[]{:S(2)}, u32[]{:S(2)}) collective-permute-start(bf16[1,1,24,3072]{3,2,0,1:T(8,128)(2,1)S(1)} %constant_dynamic-slice_fusion.1), channel_id=1, source_target_pairs={{0,16},{1,17},{2,18},{3,19},{4,20},{5,21},{6,22},{7,23},{8,24},{9,... | collective-permute-start | bytes 442376 | tf_op jit(solution)/shard_map/ppermute | solution.py:94
  239.8 17.8 %collective-permute-start.24 = (bf16[8,1,24,1536]{3,2,0,1:T(8,128)(2,1)S(1)}, bf16[8,1,24,1536]{3,2,0,1:T(8,128)(2,1)S(1)}, u32[]{:S(2)}, u32[]{:S(2)}) collective-permute-start(bf16[8,1,24,1536]{3,2,0,1:T(8,128)(2,1)S(1)} %dynamic-slice_bitcast_fusion.4), channel_id=1, source_target_pairs={{0,2},{1,3},{2,0},{3,1},{4,6},{5,7},{6,4},{7,5},{8,10},{9,11},{10,... | collective-permute-start | bytes 1769480 | tf_op jit(solution)/shard_map/ppermute | solution.py:94
  241.9 18.9 %collective-permute-start.21 = (bf16[4,2,24,1536]{3,2,1,0:T(8,128)(2,1)S(1)}, bf16[4,2,24,1536]{3,2,1,0:T(8,128)(2,1)S(1)}, u32[]{:S(2)}, u32[]{:S(2)}) collective-permute-start(bf16[4,2,24,1536]{3,2,1,0:T(8,128)(2,1)S(1)} %dynamic-slice_bitcast_fusion.5), channel_id=1, source_target_pairs={{0,4},{1,5},{2,6},{3,7},{4,0},{5,1},{6,2},{7,3},{8,12},{9,13},{10,... | collective-permute-start | bytes 1769480 | tf_op jit(solution)/shard_map/ppermute | solution.py:94
  257.7 8.7 %collective-permute-start.25 = (bf16[4,1,24,1536]{3,2,0,1:T(8,128)(2,1)S(1)}, bf16[4,1,24,1536]{3,2,0,1:T(8,128)(2,1)S(1)}, u32[]{:S(2)}, u32[]{:S(2)}) collective-permute-start(bf16[4,1,24,1536]{3,2,0,1:T(8,128)(2,1)S(1)} %dynamic-slice_bitcast_fusion.10), channel_id=1, source_target_pairs={{0,4},{1,5},{2,6},{3,7},{4,0},{5,1},{6,2},{7,3},{8,12},{9,13},{10,... | collective-permute-start | bytes 884744 | tf_op jit(solution)/shard_map/ppermute | solution.py:94
  260.9 10.7 %collective-permute-start.22 = (bf16[4,1,24,1536]{3,2,1,0:T(8,128)(2,1)S(1)}, bf16[4,1,24,1536]{3,2,1,0:T(8,128)(2,1)S(1)}, u32[]{:S(2)}, u32[]{:S(2)}) collective-permute-start(bf16[4,1,24,1536]{3,2,1,0:T(8,128)(2,1)S(1)} %constant_dynamic-slice_fusion.3), channel_id=1, source_target_pairs={{0,2},{1,3},{2,0},{3,1},{4,6},{5,7},{6,4},{7,5},{8,10},{9,11},{10,... | collective-permute-start | bytes 884744 | tf_op jit(solution)/shard_map/ppermute | solution.py:94
  271.8 7.7 %collective-permute-start.26 = (bf16[2,1,24,3072]{3,2,0,1:T(8,128)(2,1)S(1)}, bf16[2,1,24,3072]{3,2,0,1:T(8,128)(2,1)S(1)}, u32[]{:S(2)}, u32[]{:S(2)}) collective-permute-start(bf16[2,1,24,3072]{3,2,0,1:T(8,128)(2,1)S(1)} %fusion.21), channel_id=1, source_target_pairs={{0,8},{1,9},{2,10},{3,11},{4,12},{5,13},{6,14},{7,15},{8,0},{9,1},... | collective-permute-start | bytes 884744 | tf_op jit(solution)/shard_map/ppermute | solution.py:94
  279.6 7.7 %collective-permute-start.27 = (bf16[1,1,24,3072]{3,2,0,1:T(8,128)(2,1)S(1)}, bf16[1,1,24,3072]{3,2,0,1:T(8,128)(2,1)S(1)}, u32[]{:S(2)}, u32[]{:S(2)}) collective-permute-start(bf16[1,1,24,3072]{3,2,0,1:T(8,128)(2,1)S(1)} %constant_dynamic-slice_fusion.2), channel_id=1, source_target_pairs={{0,16},{1,17},{2,18},{3,19},{4,20},{5,21},{6,22},{7,23},{8,24},{9,... | collective-permute-start | bytes 442376 | tf_op jit(solution)/shard_map/ppermute | solution.py:94
  281.4 47.7 %copy-start.1 = (f32[32,12]{0,1:T(8,128)S(1)}, f32[32,12]{0,1:T(8,128)}, u32[]{:S(2)}) copy-start(f32[32,12]{0,1:T(8,128)} %param.38) | copy-start | bytes 4612
Sparse Core Ops, SparseCore 0:
  11.0 109.2 all-gather.1
  186.8 140.4 reduce-scatter.1
